TPU v7x, 256 devices: a whole 4x4x8 slice. The times are simulated.
256 devices in a mesh: pulse: 16 (over z, core), sample: 16 (over y, x).
Axes of the slice: x: 4, y: 4, z: 8, core: 2. Of those that a mesh axis runs over, the one named last changes fastest.
Arguments:
- echoes: bfloat16 [16384, 32768], P('pulse', 'sample'), may hold values from -40 to 40
- chirp_phase: float32 [16384], replicated, may hold values from -3.140625 to 3.140625
- sample_init: bfloat16 [32768, 64], P('sample'), may hold values from -0.03125 to 0.03125
- threshold: float32 [1], replicated, may hold values from 1 to 2
- ridge_scale: float32 [1], replicated, may hold values from 0.05 to 0.5
Outputs:
- doppler: float32 [256, 2, 32768], P('pulse', None, 'sample')
- rfi_pulses: float32 [16384, 64], P('pulse')
- sparse: bfloat16 [16384, 32768], P('pulse', 'sample')
All inputs are finite; a program needn't handle non-finite values.
Results may differ from a plain program's by a relative error of at most 0.0075.
Values may be sent and summed in bfloat16 or wider, within the bound.
No kernel may reach another device: no remote copies, remote signals or barrier semaphores. Data moves between devices by JAX's collectives and lax.ppermute only.
A program may use at most 64 MiB of HBM per device.

v0:
```python
import jax
import jax.numpy as jnp
from jax import lax
from jax.sharding import PartitionSpec as P

BINS = 256
ITERS = 2


def ridge(partial_sum, gram, ridge_scale):
    width = gram.shape[0]
    shift = ridge_scale[0] * jnp.trace(gram) / width
    system = gram + shift * jnp.eye(width, dtype=jnp.float32)
    factor = jnp.linalg.cholesky(system)
    return jax.scipy.linalg.cho_solve((factor, True), partial_sum.T).T


def build_kernel(bins, pulses, phases, pulse_total):
    index = jnp.mod(bins[:, None] * pulses[None, :], pulse_total)
    theta = 2.0 * jnp.pi * index.astype(jnp.float32) / pulse_total + phases[None, :]
    scale = 1.0 / jnp.sqrt(jnp.float32(pulse_total))
    kernel = (jnp.stack([jnp.cos(theta), -jnp.sin(theta)], axis=1) * scale).astype(jnp.bfloat16)
    return kernel.reshape(bins.shape[0] * 2, pulses.shape[0])


def on_device(echoes, chirp_phase, sample_init, threshold, ridge_scale):
    echo_float = echoes.astype(jnp.float32)
    pulse_groups = lax.axis_size("pulse")
    sample_groups = lax.axis_size("sample")
    rows_here, cols_here = echoes.shape
    total_cells = rows_here * cols_here * pulse_groups * sample_groups
    sample_bf = sample_init
    sparse_part = jnp.zeros(echo_float.shape, jnp.float32)
    for turn_index in range(ITERS):
        cleaned = (echo_float - sparse_part).astype(jnp.bfloat16)
        pulse_partial = jnp.dot(cleaned, sample_bf, preferred_element_type=jnp.float32)
        pulse_gram = jnp.einsum(
            "sr,sq->rq", sample_bf, sample_bf, preferred_element_type=jnp.float32
        )
        pulse_partial, pulse_gram = lax.psum((pulse_partial, pulse_gram), "sample")
        pulse_factor = ridge(pulse_partial, pulse_gram, ridge_scale)
        pulse_bf = pulse_factor.astype(jnp.bfloat16)
        sample_partial = jnp.einsum(
            "ps,pr->sr", cleaned, pulse_bf, preferred_element_type=jnp.float32
        )
        sample_gram = jnp.einsum(
            "pr,pq->rq", pulse_bf, pulse_bf, preferred_element_type=jnp.float32
        )
        sample_partial, sample_gram = lax.psum((sample_partial, sample_gram), "pulse")
        sample_bf = ridge(sample_partial, sample_gram, ridge_scale).astype(jnp.bfloat16)
        low_rank = jnp.einsum("pr,sr->ps", pulse_bf, sample_bf, preferred_element_type=jnp.float32)
        residual = echo_float - low_rank
        square_sum = lax.psum(jnp.sum(residual * residual), ("pulse", "sample"))
        level = threshold[0] * jnp.sqrt(square_sum / total_cells + 1e-06)
        sparse_part = residual - jnp.clip(residual, -level, level)
    clean_bf = residual.astype(jnp.bfloat16)
    pulse_total = rows_here * pulse_groups
    bins_here = BINS // pulse_groups
    first_row = lax.axis_index("pulse") * rows_here
    pulses = first_row + jnp.arange(rows_here, dtype=jnp.int32)
    phases = lax.dynamic_slice_in_dim(chirp_phase, first_row, rows_here)
    bins = jnp.arange(bins_here * lax.axis_size("pulse"), dtype=jnp.int32) - BINS // 2
    kernel = build_kernel(bins, pulses, phases, pulse_total)
    product = jnp.dot(kernel, clean_bf, preferred_element_type=jnp.float32)
    doppler = lax.psum_scatter(
        product.reshape(bins_here * lax.axis_size("pulse"), 2, cols_here),
        "pulse",
        scatter_dimension=0,
        tiled=True,
    )
    return (doppler, pulse_factor, sparse_part.astype(jnp.bfloat16))


def solution(mesh):
    placed = (P("pulse", "sample"), P(), P("sample", None), P(), P())
    return jax.shard_map(
        on_device,
        mesh=mesh,
        in_specs=placed,
        out_specs=(P("pulse", None, "sample"), P("pulse", None), P("pulse", "sample")),
        check_vma=False,
    )
```

profile of v0, /device:TPU:1, one launch (start us, length us, event | category | flops | bytes accessed | tf_op | source)
XLA Modules:
  0.0 642.0 jit_solution(17133276551477953953)
XLA Ops:
  8.1 4.3 fusion.44
  12.7 61.2 %psum.70 = f32[64,64]{0,1:T(8,128)S(1)} all-reduce(f32[64,64]{0,1:T(8,128)S(1)} %fusion.43), channel_id=1, replica_groups=mesh['pulse'=16,'sample'=16] {'sample'}, use_global_device_ids=true, to_apply=%region_0.0 | all-reduce | flops 4096 | bytes 32768 | tf_op jit(solution)/shard_map/psum | solution.py:40
  76.0 5.8 cholesky.74
  83.2 4.9 custom-call.14
  93.7 16.0 %all-reduce.5.cloned.1.call-done = f32[64,1024]{1,0:T(8,128)} async-done(((f32[64,1024]{1,0:T(8,128)}), f32[64,1024]{1,0:T(8,128)}) %all-reduce.5.cloned.1.call-update) | async-done | bytes 262160 | tf_op jit(solution)/shard_map/psum | solution.py:40
  115.5 45.6 %psum.72 = f32[64,64]{0,1:T(8,128)S(1)} all-reduce(f32[64,64]{0,1:T(8,128)S(1)} %fusion.45), channel_id=1, replica_groups=mesh['pulse'=16,'sample'=16] {'pulse'}, use_global_device_ids=true, to_apply=%region_5.8 | all-reduce | flops 4096 | bytes 32768 | tf_op jit(solution)/shard_map/psum | solution.py:49
  162.4 5.8 cholesky.85
  169.6 4.9 custom-call.15
  174.5 53.4 %all-reduce.7.cloned.1.call-done = f32[64,2048]{1,0:T(8,128)} async-done(((f32[64,2048]{1,0:T(8,128)}), f32[64,2048]{1,0:T(8,128)}) %all-reduce.7.cloned.1.call-update) | async-done | bytes 524304 | tf_op jit(solution)/shard_map/psum | solution.py:49
  230.2 7.3 %multiply_reduce_fusion.1 = (f32[]{:T(128)}, f32[1024,2048]{1,0:T(8,128)}) fusion(bf16[1024,2048]{1,0:T(8,128)(2,1)} %param.10, bf16[64,1024]{1,0:T(8,128)(2,1)S(1)} %convolution_convert_fusion.2, bf16[64,2048]{1,0:T(8,128)(2,1)S(1)} %convolution_convert_fusion.1), kind=kOutput, calls=%fused_computation.6 | convolution fusion | flops 276824064 | bytes 12976132 | tf_op jit(solution)/shard_map/pr,sr->ps/dot_general | solution.py:51
  237.7 77.8 %psum.75 = f32[]{:T(128)} all-reduce(f32[]{:T(128)} %get-tuple-element.11), channel_id=1, replica_groups=mesh['pulse'=16,'sample'=16] {'pulse','sample'}, use_global_device_ids=true, to_apply=%region_11.15 | all-reduce | flops 1 | bytes 8 | tf_op jit(solution)/shard_map/psum | solution.py:53
  316.2 5.6 fusion
  326.0 57.0 %psum.74 = f32[64,64]{0,1:T(8,128)S(1)} all-reduce(f32[64,64]{0,1:T(8,128)S(1)} %fusion.47), channel_id=1, replica_groups=mesh['pulse'=16,'sample'=16] {'sample'}, use_global_device_ids=true, to_apply=%region_8.12 | all-reduce | flops 4096 | bytes 32768 | tf_op jit(solution)/shard_map/psum | solution.py:40
  384.4 5.8 cholesky.96
  391.6 4.9 custom-call.16
  396.5 17.9 %all-reduce.9.cloned.1.call-done = f32[64,1024]{1,0:T(8,128)} async-done(((f32[64,1024]{1,0:T(8,128)}), f32[64,1024]{1,0:T(8,128)}) %all-reduce.9.cloned.1.call-update) | async-done | bytes 262160 | tf_op jit(solution)/shard_map/psum | solution.py:40
  420.3 45.3 %psum.77 = f32[64,64]{0,1:T(8,128)S(1)} all-reduce(f32[64,64]{0,1:T(8,128)S(1)} %fusion.40), channel_id=1, replica_groups=mesh['pulse'=16,'sample'=16] {'pulse'}, use_global_device_ids=true, to_apply=%region_13.17 | all-reduce | flops 4096 | bytes 32768 | tf_op jit(solution)/shard_map/psum | solution.py:49
  467.0 5.8 cholesky.107
  474.2 4.9 custom-call.17
  479.1 53.7 %all-reduce.11.cloned.1.call-done = f32[64,2048]{1,0:T(8,128)} async-done(((f32[64,2048]{1,0:T(8,128)}), f32[64,2048]{1,0:T(8,128)}) %all-reduce.11.cloned.1.call-update) | async-done | bytes 524304 | tf_op jit(solution)/shard_map/psum | solution.py:49
  535.1 5.2 multiply_reduce_fusion
  543.4 4.4 fusion.1
  547.9 78.2 %psum.79 = f32[]{:T(128)} all-reduce(f32[]{:T(128)} %get-tuple-element.13), channel_id=1, replica_groups=mesh['pulse'=16,'sample'=16] {'pulse','sample'}, use_global_device_ids=true, to_apply=%region_18.22 | all-reduce | flops 1 | bytes 8 | tf_op jit(solution)/shard_map/psum | solution.py:53
  626.8 6.8 %subtract_convert_fusion = bf16[1024,2048]{1,0:T(8,128)(2,1)} fusion(f32[1024,2048]{1,0:T(8,128)} %copy-done.1, f32[]{:T(128)S(6)} %neg.18, f32[]{:T(128)S(6)} %mul.108), kind=kLoop, calls=%fused_computation.4 | loop fusion | flops 8388608 | bytes 12582920 | tf_op jit(solution)/shard_map/convert_element_type | solution.py:71
  (67 shorter events, 40.0 us)
Async XLA Ops:
  7.2 1.0 copy-start
  7.2 102.5 %all-reduce.5.cloned.1.call-start = ((), (), s32[]{:S(2)}) async-start(), calls=%async_computation.1 | async-start | bytes 524288 | tf_op jit(solution)/shard_map/psum | solution.py:40
  12.4 215.5 %all-reduce.7.cloned.1.call-start = ((), (), s32[]{:S(2)}) async-start(), calls=%async_computation.2 | async-start | bytes 1048576 | tf_op jit(solution)/shard_map/psum | solution.py:49
  115.4 298.9 %all-reduce.9.cloned.1.call-start = ((), (), s32[]{:S(2)}) async-start(), calls=%async_computation.3 | async-start | bytes 524288 | tf_op jit(solution)/shard_map/psum | solution.py:40
  321.8 2.0 copy-start.2
  325.9 206.9 %all-reduce.11.cloned.1.call-start = ((), (), s32[]{:S(2)}) async-start(), calls=%async_computation.4 | async-start | bytes 1048576 | tf_op jit(solution)/shard_map/psum | solution.py:49
  416.1 124.1 %copy-start.3 = (f32[1024,64]{0,1:T(8,128)}, f32[1024,64]{0,1:T(8,128)S(1)}, u32[]{:S(2)}) copy-start(f32[1024,64]{0,1:T(8,128)S(1)} %convolution_bitcast_fusion) | copy-start | bytes 786436
  420.3 213.3 %reduce-scatter.2.cloned.1.call-start = ((), (), s32[]{:S(2)}) async-start(), calls=%async_computation.5 | async-start | bytes 4456448 | tf_op jit(solution)/shard_map/reduce_scatter | solution.py:65
  540.2 3.2 copy-start.1
Sparse Core Ops, SparseCore 0:
  12.6 97.0 all-reduce.4
  115.5 112.3 all-reduce.6
  326.1 88.2 all-reduce.8
  420.4 112.3 all-reduce.10
  548.0 61.1 reduce-scatter.1
where the time goes:
time: 643 us; the launch traced here: 642 us
  blocking collectives  365 us (57%)
  waiting for transfers between devices  141 us (22%)
  other arithmetic  67.5 us (10%)
  matrix products  39.7 us (6%)
  between operations  19.4 us (3%)
  local copies, waits for them, and re-layouts  8.98 us (1%)
    psum x2, blocking collectives, on_device(): square_sum = lax.psum(jnp.sum(residual * residual), ('pulse', 'sample'))  156 us
    psum x2, blocking collectives, on_device(): pulse_partial, pulse_gram = lax.psum((pulse_partial, pulse_gram), 'sample')  118 us
    psum x2, waiting for transfers between devices, on_device(): lax.psum((sample_partial, sample_gram), 'pulse')  107 us
    psum x2, blocking collectives, on_device(): lax.psum((sample_partial, sample_gram), 'pulse')  90.9 us
    psum x2, waiting for transfers between devices, on_device(): pulse_partial, pulse_gram = lax.psum((pulse_partial, pulse_gram), 'sample')  33.8 us
    another operation x12, other arithmetic, ridge(): factor = jnp.linalg.cholesky(system)  26.1 us
    another operation x8, other arithmetic, ridge(): return jax.scipy.linalg.cho_solve((factor, True), partial_sum.T).T  22.2 us
  transfers between devices with their start and end apart: 5, of which 4 were waited for; matrix products, arithmetic and copies ran while one was open for 10% of the time, Pallas kernels for 0%

commit v1 on v0

v1 whole, which is shorter than its diff:
```python
import jax
import jax.numpy as jnp
from jax import lax
from jax.experimental import pallas as pl
from jax.experimental.pallas import tpu as pltpu
from jax.sharding import PartitionSpec as P


BINS = 256
ITERS = 2
RANK = 64
F32 = jnp.float32
BF16 = jnp.bfloat16
HIGH = lax.Precision.HIGHEST

NN = (((1,), (0,)), ((), ()))
NT = (((1,), (1,)), ((), ()))


def mm(a, b, dims):
    return lax.dot_general(a, b, dims, preferred_element_type=F32)


def mm_exact(a, b):
    return lax.dot_general(a, b, NN, precision=HIGH, preferred_element_type=F32)


def lanes_low(shape):
    return lax.broadcasted_iota(jnp.int32, shape, 1) < RANK


def pack_square(twice):
    half = RANK // 2
    return jnp.where(lanes_low((half, 128)), twice[:half], twice[half:])


def unpack_square(packed):
    swapped = pltpu.roll(packed, RANK, 1)
    low = lanes_low(packed.shape)
    return jnp.concatenate(
        [jnp.where(low, packed, swapped), jnp.where(low, swapped, packed)], axis=0
    )


def ridge_inverse(twice, ridge_scale):
    row = lax.broadcasted_iota(jnp.int32, (RANK, 128), 0)
    lane = lax.broadcasted_iota(jnp.int32, (RANK, 128), 1)
    diag = row == lane
    trace = jnp.sum(jnp.sum(jnp.where(diag, twice, 0.0), axis=0, keepdims=True), axis=1, keepdims=True)
    shift = ridge_scale * trace / RANK
    unit = (lane == row + RANK).astype(F32)
    work = jnp.where(lane < RANK, twice + jnp.where(diag, shift, 0.0), unit)
    panel = 8
    for start in range(0, RANK, panel):
        columns = [
            jnp.broadcast_to(work[:, start + j : start + j + 1], (RANK, 128)) for j in range(panel)
        ]
        for j in range(panel):
            k = start + j
            inverse = 1.0 / columns[j][k : k + 1, :]
            scaled = work[k : k + 1, :] * inverse
            for i in range(j + 1, panel):
                entry = columns[j][start + i : start + i + 1, :] * inverse
                columns[i] = jnp.where(row == k, entry, columns[i] - columns[j] * entry)
            work = jnp.where(row == k, scaled, work - columns[j] * scaled)
    swapped = pltpu.roll(work, RANK, 1)
    return jnp.where(lane < RANK, swapped, work)


def stack_factor(v_ref, va_ref, vb_ref, ta_ref=None, tb_ref=None):
    chunks, rank, width = v_ref.shape
    cols = chunks * width
    va_ref[rank:, :] = jnp.zeros((rank, cols), va_ref.dtype)
    vb_ref[:rank, :] = jnp.zeros((rank, cols), vb_ref.dtype)
    for j in range(chunks):
        part = v_ref[j]
        here = slice(j * width, (j + 1) * width)
        va_ref[:rank, here] = part
        vb_ref[rank:, here] = part
        if ta_ref is not None:
            turned = jnp.concatenate([part, part], axis=0).T
            zero = jnp.zeros_like(turned)
            low = lanes_low(turned.shape)
            ta_ref[here, :] = jnp.where(low, turned, zero)
            tb_ref[here, :] = jnp.where(low, zero, turned)


def first_products(echo_ref, v_ref, out_ref, ta, tb, gram):
    @pl.when(pl.program_id(0) == 0)
    def _():
        factor = v_ref[...]
        both = jnp.concatenate([factor, factor], axis=0)
        gram[...] = pack_square(mm(factor, both, NT))
        width = 256
        low = lanes_low((width, 128))
        zero = jnp.zeros((width, 128), BF16)
        for j in range(ta.shape[0] // width):
            here = slice(j * width, (j + 1) * width)
            turned = both[:, here].T
            ta[here, :] = jnp.where(low, turned, zero)
            tb[here, :] = jnp.where(low, zero, turned)

    part = mm(echo_ref[0], ta[...], NN) + mm(echo_ref[1], tb[...], NN)
    out_ref[:, :32, :] = part.reshape(out_ref.shape[0], 32, 128)
    out_ref[:, 32:, :] = jnp.broadcast_to(gram[...][None], (out_ref.shape[0], 32, 128))


def level_of(sums, threshold, cells):
    tile = jnp.sum(sums, axis=0)
    total = jnp.sum(jnp.sum(tile, axis=0, keepdims=True), axis=1, keepdims=True)
    return threshold * jnp.sqrt(total / cells + 1e-06)


def next_products(cells, scalars, echo_ref, u_ref, v_ref, sums_ref, out_ref, clean_ref, va, vb, ta, tb, buffer, sems):
    stack_factor(v_ref, va, vb, ta, tb)
    copies = []
    level = level_of(sums_ref[...], scalars[0:1, 0:1], cells)
    rows = u_ref.shape[0] // 2
    for i in range(2):
        here = slice(i * rows, (i + 1) * rows)
        part = None
        for h, stacked, turned in ((0, va, ta), (1, vb, tb)):
            echo = echo_ref[h, here].astype(F32)
            residual = echo - mm(u_ref[here], stacked[...], NN)
            sparse = residual - jnp.clip(residual, -level, level)
            cleaned = (echo - sparse).astype(BF16)
            buffer[h, i] = cleaned
            copy = pltpu.make_async_copy(buffer.at[h, i], clean_ref.at[h, pl.ds(i * rows, rows)], sems.at[h, i])
            copy.start()
            copies.append(copy)
            term = mm(cleaned, turned[...], NN)
            part = term if part is None else part + term
        out_ref[8 * i : 8 * (i + 1)] = part.reshape(8, 32, 128)
    for copy in copies:
        copy.wait()


def inverse_block(twice, ridge_scale):
    inverse = ridge_inverse(twice, ridge_scale)
    low = lanes_low((RANK, 128))
    return jnp.concatenate([jnp.where(low, inverse, 0.0), jnp.where(low, 0.0, inverse)], axis=0)


def invert_gram(scalars, got_ref, out_ref):
    total = jnp.sum(got_ref[:, 8:, :], axis=0)
    out_ref[...] = inverse_block(unpack_square(total), scalars[1:2, 0:1])


def solve_pulses(scalars, got_ref, out_ref):
    total = jnp.sum(got_ref[...], axis=0)
    block = inverse_block(unpack_square(total[32:]), scalars[1:2, 0:1])
    factor = mm_exact(total[:32], block).astype(out_ref.dtype)
    out_ref[...] = jnp.broadcast_to(factor[None], out_ref.shape)


def apply_pulses(got_ref, block_ref, out_ref):
    factor = mm_exact(jnp.sum(got_ref[...], axis=0), block_ref[...]).astype(out_ref.dtype)
    out_ref[...] = jnp.broadcast_to(factor[None], out_ref.shape)


def solve_samples(scalars, got_ref, out_ref, *rest):
    total = jnp.sum(got_ref[...], axis=0)
    inverse = ridge_inverse(unpack_square(total[RANK : RANK + 32]), scalars[1:2, 0:1])
    factor = mm_exact(inverse[:, :RANK], total[:RANK]).astype(out_ref.dtype)
    out_ref[...] = jnp.broadcast_to(factor[None], out_ref.shape)
    if rest:
        rest[0][...] = total[RANK + 32 :]


def sample_products(data_ref, u_ref, *refs):
    kernel_ref = refs[0] if len(refs) == 4 else None
    keep_ref, send_ref, turned = refs[-3:]
    width = 128
    own = lax.axis_index("pulse") % 2 == 0

    @pl.when(pl.program_id(0) == 0)
    def _():
        turned[...] = u_ref[...].T

    square = mm(turned[...], u_ref[...], NN)
    mixed = jnp.where(lanes_low((RANK, 128)), square[:RANK], square[RANK:])
    gram = pack_square(mixed + pltpu.roll(mixed, RANK, 1))
    product = mm(turned[:RANK], data_ref[0], NN) + mm(turned[RANK:], data_ref[1], NN)
    chunks = keep_ref.shape[0]
    for z in range(chunks):
        zero = product[:, 2 * z * width : (2 * z + 1) * width]
        one = product[:, (2 * z + 1) * width : (2 * z + 2) * width]
        keep_ref[z, :RANK, :] = jnp.where(own, zero, one)
        send_ref[z, :RANK, :] = jnp.where(own, one, zero)
        keep_ref[z, RANK : RANK + 32, :] = gram
        send_ref[z, RANK : RANK + 32, :] = gram
    if kernel_ref is not None:
        half = kernel_ref.shape[1] // 2
        low = lanes_low((kernel_ref.shape[0], 128))
        mixed = jnp.where(
            low, mm(kernel_ref[:, :half], u_ref[...], NN), mm(kernel_ref[:, half:], u_ref[...], NN)
        )
        twice = mixed + pltpu.roll(mixed, RANK, 1)
        low = lanes_low((16, 128))
        for z in range(chunks):
            mine = twice[64 * z : 64 * (z + 1)]
            zero = jnp.where(low, mine[:16], mine[16:32])
            one = jnp.where(low, mine[32:48], mine[48:])
            keep_ref[z, RANK + 32 :, :] = jnp.where(own, zero, one)
            send_ref[z, RANK + 32 :, :] = jnp.where(own, one, zero)


def residual_squares(with_gram, echo_ref, u_ref, v_ref, out_ref, va, vb):
    stack_factor(v_ref, va, vb)
    rows = u_ref.shape[0] // 2
    total = jnp.zeros((8, va.shape[1]), F32)
    for i in range(2):
        here = slice(i * rows, (i + 1) * rows)
        for h, stacked in ((0, va), (1, vb)):
            residual = echo_ref[h, here].astype(F32) - mm(u_ref[here], stacked[...], NN)
            square = residual * residual
            total = total + jnp.sum(square.reshape(-1, 8, square.shape[1]), axis=0)
    tile = total[:, :128]
    for j in range(1, total.shape[1] // 128):
        tile = tile + total[:, 128 * j : 128 * (j + 1)]
    if with_gram:
        square = mm(va[:RANK, :], va[...] + vb[...], NT)
        tile = jnp.concatenate([tile, pack_square(square)], axis=0)
    out_ref[...] = jnp.broadcast_to(tile[None], out_ref.shape)


def correct_doppler(v_ref, dop_ref, ku_ref, dop_out):
    ku = ku_ref[...]
    high = ku.astype(BF16)
    rest = ku - high.astype(F32)
    middle = rest.astype(BF16)
    low = (rest - middle.astype(F32)).astype(BF16)
    chunks, _, width = v_ref.shape
    zero = jnp.zeros((16, RANK), BF16)
    parts = []
    for part in (high, middle, low):
        parts += [part[:, :RANK], part[:, RANK:]]
    parts = jnp.concatenate(parts, axis=0)
    for j in range(chunks):
        here = slice(j * width, (j + 1) * width)
        fix = mm(parts, v_ref[j], NN)
        fix = fix[:32] + (fix[32:64] + fix[64:])
        value = dop_ref[0, :, here] - fix
        dop_out[:, 0, here] = value[:16]
        dop_out[:, 1, here] = value[16:]


def finish(cells, scalars, echo_ref, u_ref, v_ref, sums_ref, sparse_ref, va, vb, level_ref):
    @pl.when(pl.program_id(0) == 0)
    def _():
        stack_factor(v_ref, va, vb)
        level_ref[...] = jnp.broadcast_to(level_of(sums_ref[...], scalars[0:1, 0:1], cells), (1, 128))

    level = level_ref[0:1, 0:1]
    rows = echo_ref.shape[1]
    u = u_ref[pl.ds(pl.multiple_of(pl.program_id(0) * rows, rows), rows), :]
    for h, stacked in ((0, va), (1, vb)):
        residual = echo_ref[h].astype(F32) - mm(u, stacked[...], NN)
        sparse_ref[h] = (residual - jnp.clip(residual, -level, level)).astype(BF16)


def doppler_products(ca_ref, sa_ref, cb_ref, sb_ref, echo_ref, kernel_ref, out_ref):
    groups = ca_ref.shape[0]

    @pl.when(pl.program_id(0) == 0)
    def _():
        cb, sb = cb_ref[...], sb_ref[...]
        for g in range(groups):
            ca, sa = ca_ref[g : g + 1, :], sa_ref[g : g + 1, :]
            kernel_ref[32 * g : 32 * g + 16, :] = (ca * cb - sa * sb).astype(BF16)
            kernel_ref[32 * g + 16 : 32 * (g + 1), :] = (-(sa * cb + ca * sb)).astype(BF16)

    out_ref[...] = mm(kernel_ref[...], echo_ref[...], NN)


def full(shape):
    return pl.BlockSpec(shape, lambda *_: (0,) * len(shape))


VMEM = pl.BlockSpec(memory_space=pltpu.VMEM)
HBM = pl.BlockSpec(memory_space=pl.ANY)


def call(body, outs, *args, scratch=(), blocked=None, blocked_out=None, steps=None, in_hbm=()):
    blocked, blocked_out = blocked or {}, blocked_out or {}
    in_specs = [blocked.get(i, VMEM) for i in range(len(args))]
    out_specs = [blocked_out.get(i, HBM if i in in_hbm else VMEM) for i in range(len(outs))]
    shapes = [
        jax.ShapeDtypeStruct(*shape) if i in blocked_out else (pltpu.HBM if i in in_hbm else pltpu.VMEM)(*shape)
        for i, shape in enumerate(outs)
    ]
    args = [
        pltpu.with_memory_space_constraint(arg, pltpu.HBM if i in blocked else pltpu.VMEM)
        for i, arg in enumerate(args)
    ]
    return pl.pallas_call(
        body, in_specs=in_specs, out_specs=out_specs, out_shape=shapes, scratch_shapes=list(scratch),
        compiler_params=pltpu.CompilerParams(vmem_limit_bytes=28 * 2**20), **({"grid": (steps,)} if steps else {}),
    )(*args)


def on_device(echoes, chirp_phase, sample_init, threshold, ridge_scale):
    groups = lax.axis_size("pulse")
    rows, cols = echoes.shape
    half = rows // 2
    cells = rows * cols * groups * lax.axis_size("sample")
    pulse_total = rows * groups
    own_pulse = lax.axis_index("pulse")
    scalars = jnp.broadcast_to(jnp.concatenate([threshold, ridge_scale] * 4)[:, None], (8, 128))
    echo3 = echoes.reshape(2, half, cols)
    across_z = [[2 * z + c for z in range(groups // 2)] for c in range(2)]
    other_core = [(i, i ^ 1) for i in range(groups)]
    stacked = [pltpu.VMEM((128, cols), BF16)] * 2
    turned = [pltpu.VMEM((cols, 128), BF16)] * 2

    bp = half // 2
    row_blocks = pl.BlockSpec((2, bp, cols), lambda i: (0, i, 0))
    to_solve = call(
        first_products, [((16, 64, 128), F32)], echo3, sample_init.T, steps=2,
        blocked={0: row_blocks}, blocked_out={0: pl.BlockSpec((8, 64, 128), lambda i: (i, 0, 0))},
        scratch=turned + [pltpu.VMEM((32, 128), F32)],
    )[0]
    to_solve, chirp_phase = lax.optimization_barrier((to_solve, chirp_phase))
    got = lax.all_to_all(to_solve, "sample", 0, 0, tiled=True)

    pulses = own_pulse * rows + jnp.arange(rows, dtype=jnp.int32)
    phases = lax.dynamic_slice_in_dim(chirp_phase, own_pulse * rows, rows)
    steps = jnp.arange(16, dtype=jnp.int32)[:, None]
    turn = 2.0 * jnp.pi / pulse_total
    angle_a = jnp.mod((16 * steps - BINS // 2) * pulses[None, :], pulse_total).astype(F32) * turn + phases[None, :]
    angle_b = jnp.mod(steps * pulses[None, :], pulse_total).astype(F32) * turn
    scale = 1.0 / jnp.sqrt(F32(pulse_total))
    table = full((16, rows))
    dcols = 512
    kernel, spectrum = pl.pallas_call(
        doppler_products, grid=(cols // dcols,),
        in_specs=[table] * 4 + [pl.BlockSpec((rows, dcols), lambda i: (0, i))],
        out_specs=[full((2 * BINS, rows)), pl.BlockSpec((2 * BINS, dcols), lambda i: (0, i))],
        out_shape=[jax.ShapeDtypeStruct((2 * BINS, rows), BF16), jax.ShapeDtypeStruct((2 * BINS, cols), F32)],
        compiler_params=pltpu.CompilerParams(vmem_limit_bytes=56 * 2**20), name="doppler_products",
    )(jnp.cos(angle_a) * scale, jnp.sin(angle_a) * scale, jnp.cos(angle_b), jnp.sin(angle_b), echoes)
    spectrum = lax.psum_scatter(
        spectrum.reshape(groups, 2 * BINS // groups, cols), "pulse", scatter_dimension=0, tiled=True
    )

    data3 = echo3
    for turn_index in range(ITERS):
        last = turn_index == ITERS - 1
        pulse_out = [((16, 32, 128), F32 if last else BF16)]
        if turn_index == 0:
            mine = call(solve_pulses, pulse_out, scalars, got)[0]
        else:
            got = lax.all_to_all(to_solve, "sample", 0, 0, tiled=True)
            block = call(invert_gram, [((128, 128), F32)], scalars, grams)[0]
            mine = call(apply_pulses, pulse_out, got, block)[0]
        u_full = lax.all_to_all(mine, "sample", 0, 0, tiled=True).reshape(half, 128)
        u_bf = u_full.astype(BF16)
        depth = RANK + 32 + (16 if last else 0)
        extra = [kernel] if last else []
        keep, send = call(
            sample_products, [((8, depth, 128), F32)] * 2, data3, u_bf, *extra, steps=2,
            blocked={0: pl.BlockSpec((2, half, cols // 2), lambda i: (0, 0, i)), 2: pl.BlockSpec((BINS, rows), lambda i: (i, 0))},
            blocked_out={i: pl.BlockSpec((4, depth, 128), lambda i: (i, 0, 0)) for i in range(2)},
            scratch=[pltpu.VMEM((128, half), BF16)],
        )
        keep = keep + lax.ppermute(send, "pulse", other_core)
        got = lax.all_to_all(keep, "pulse", 0, 0, tiled=True, axis_index_groups=across_z)
        outs = [((16, RANK, 128), BF16)] + ([((16, 128), F32)] if last else [])
        mine = call(solve_samples, outs, scalars, got)
        v_chunks = lax.all_to_all(mine[0], "pulse", 0, 0, tiled=True)
        height = 8 if last else 40
        grams = call(
            lambda *refs: residual_squares(not last, *refs), [((16, height, 128), F32)],
            echo3, u_bf, v_chunks, scratch=stacked,
        )[0]
        grams = lax.all_to_all(grams, "sample", 0, 0, tiled=True)
        sums = jnp.sum(grams[:, :8], axis=0, keepdims=True)
        if last:
            sums, spectrum = lax.optimization_barrier((sums, spectrum))
        sums = lax.all_to_all(jnp.broadcast_to(sums, (16, 8, 128)), "pulse", 0, 0, tiled=True)
        if not last:
            to_solve, data3 = call(
                lambda *refs: next_products(cells, *refs),
                [((16, 32, 128), F32), (echo3.shape, BF16)],
                scalars, echo3, u_bf, v_chunks, sums, in_hbm=(1,),
                scratch=stacked + turned + [pltpu.VMEM((2, 2, bp, cols), BF16), pltpu.SemaphoreType.DMA((2, 2))],
            )
    doppler = call(correct_doppler, [((16, 2, cols), F32)], v_chunks, spectrum, mine[1])[0]
    sums, doppler = lax.optimization_barrier((sums, doppler))
    sparse = call(
        lambda *refs: finish(cells, *refs), [(echo3.shape, BF16)],
        scalars, echo3, u_bf, v_chunks, sums, steps=2, blocked={1: row_blocks}, blocked_out={0: row_blocks},
        scratch=stacked + [pltpu.VMEM((1, 128), F32)],
    )[0]
    turned_factor = u_full.T
    pulse_factor = jnp.concatenate([turned_factor[:RANK], turned_factor[RANK:]], axis=1).T
    return (doppler, pulse_factor, sparse.reshape(rows, cols))


def solution(mesh):
    placed = (P("pulse", "sample"), P(), P("sample", None), P(), P())
    return jax.shard_map(
        on_device,
        mesh=mesh,
        in_specs=placed,
        out_specs=(P("pulse", None, "sample"), P("pulse", None), P("pulse", "sample")),
        check_vma=False,
    )
```

time: 643 us -> 236 us (0.37)
  blocking collectives: 365 us -> 119 us
  waiting for transfers between devices: 141 us -> 31.1 us
  other arithmetic: 67.5 us -> 1.44 us
  matrix products: 39.7 us -> 0 us
  Pallas kernels: 0 us -> 39.5 us
  starting transfers between devices: 0.21 us -> 23.7 us
    psum x6 -> x0, blocking collectives: 365 us -> none  [the longest x2 156 us: on_device(): square_sum = lax.psum(jnp.sum(residual * residual), ('pulse', 'sample'))]
    psum x4 -> x0, waiting for transfers between devices: 141 us -> none  [the longest x2 107 us: on_device(): lax.psum((sample_partial, sample_gram), 'pulse')]
    all_to_all x0 -> x8, blocking collectives: none -> 119 us  [the longest x2 40.8 us: on_device(): lax.all_to_all(keep, 'pulse', 0, 0, tiled=True, axis_index_groups=across_z)]
    another operation x20 -> x0, other arithmetic: 48.3 us -> none  [the longest x12 26.1 us: ridge(): factor = jnp.linalg.cholesky(system)]
    pallas_call x0 -> x14, Pallas kernels: none -> 39.5 us  [the longest x13 33.1 us: call(): pl.pallas_call(body, in_specs=in_specs, out_specs=out_specs, out_shape=sh...]
    dot_general x11 -> x0, matrix products: 31.8 us -> none  [the longest x2 12.5 us: on_device(): jnp.einsum('pr,sr->ps', pulse_bf, sample_bf, preferred_element_type=jnp.f...]
    all_to_all x0 -> x4, waiting for transfers between devices: none -> 28.1 us  [the longest x2 15.8 us: on_device(): got = lax.all_to_all(to_solve, 'sample', 0, 0, tiled=True)]
    all_to_all x0 -> x4, starting transfers between devices: none -> 18.3 us  [the longest x2 11.1 us: on_device(): got = lax.all_to_all(to_solve, 'sample', 0, 0, tiled=True)]
  transfers between devices with their start and end apart: 5 -> 7, of which waited for: 4 -> 6; matrix products, arithmetic and copies ran while one was open for 10% -> 1% of each run, Pallas kernels for 0% -> 10%
where the time goes in v1:
time: 236 us; the launch traced here: 235 us
  blocking collectives  119 us (50%)
  Pallas kernels  39.5 us (17%)
  waiting for transfers between devices  31.1 us (13%)
  starting transfers between devices  23.7 us (10%)
  between operations  15.5 us (7%)
  local copies, waits for them, and re-layouts  5.11 us (2%)
    all_to_all x2, blocking collectives, on_device(): lax.all_to_all(keep, 'pulse', 0, 0, tiled=True, axis_index_groups=across_z)  40.8 us
    pallas_call x13, Pallas kernels, call(): pl.pallas_call(body, in_specs=in_specs, out_specs=out_specs, out_shape=sh...  33.1 us
    all_to_all x2, blocking collectives, on_device(): v_chunks = lax.all_to_all(mine[0], 'pulse', 0, 0, tiled=True)  31.4 us
    all_to_all x2, blocking collectives, on_device(): u_full = lax.all_to_all(mine, 'sample', 0, 0, tiled=True).reshape(half, 128)  20.6 us
    all_to_all x2, waiting for transfers between devices, on_device(): got = lax.all_to_all(to_solve, 'sample', 0, 0, tiled=True)  15.8 us
    all_to_all x1, blocking collectives, on_device(): grams = lax.all_to_all(grams, 'sample', 0, 0, tiled=True)  13.8 us
    all_to_all x1, blocking collectives, on_device(): lax.all_to_all(jnp.broadcast_to(sums, (16, 8, 128)), 'pulse', 0, 0, tiled...  12 us
    all_to_all x2, starting transfers between devices, on_device(): got = lax.all_to_all(to_solve, 'sample', 0, 0, tiled=True)  11.1 us
  transfers between devices with their start and end apart: 7, of which 6 were waited for; matrix products, arithmetic and copies ran while one was open for 1% of the time, Pallas kernels for 10%

profile of v1, /device:TPU:1, one launch (start us, length us, event | category | flops | bytes accessed | tf_op | source)
XLA Modules:
  0.0 234.8 jit_solution(734032436657230935)
XLA Ops:
  8.2 4.0 %shard_map.76 = f32[16,64,128]{2,1,0:T(8,128)} custom-call(bf16[2,512,2048]{2,1,0:T(8,128)(2,1)} %bitcast.13, bf16[64,2048]{1,0:T(8,128)(2,1)S(1)} %bitcast.22), custom_call_target="tpu_custom_call" | custom-call | tf_op jit(solution)/shard_map/pallas_call | solution.py:296
  14.1 6.4 %doppler_products.1 = (bf16[512,1024]{1,0:T(8,128)(2,1)}, f32[512,2048]{1,0:T(8,128)}) custom-call(f32[16,1024]{1,0:T(8,128)} %get-tuple-element.41.ca_ref, f32[16,1024]{1,0:T(8,128)} %get-tuple-element.40.sa_ref, f32[16,1024]{1,0:T(8,128)} %get-tuple-element.43.cb_ref, f32[16,1024]{1,0:T(8,128)} %get-tuple-element.42.sb_ref, bf16[1024,2048]{1,0:T(8,128)(2,1)} %echo_ref.1), custom_call_target="tpu_custom_call" | custom-call | tf_op jit(solution)/shard_map/doppler_products/pallas_call | solution.py:335
  20.6 7.6 %all-to-all-start = ((f32[16,64,128]{2,1,0:T(8,128)}), f32[16,64,128]{2,1,0:T(8,128)S(1)}, u32[]{:S(2)}, u32[]{:S(2)}) async-start(f32[16,64,128]{2,1,0:T(8,128)} %shard_map.76), calls=%async_computation | async-start | bytes 1048576 | tf_op jit(solution)/shard_map/all_to_all | solution.py:324
  29.5 9.0 %all-to-all-done.got_ref = f32[16,64,128]{2,1,0:T(8,128)S(1)} async-done(((f32[16,64,128]{2,1,0:T(8,128)}), f32[16,64,128]{2,1,0:T(8,128)S(1)}, u32[]{:S(2)}, u32[]{:S(2)}) %all-to-all-start) | async-done | bytes 524320 | tf_op jit(solution)/shard_map/all_to_all | solution.py:324
  40.9 10.1 %all_to_all.60 = bf16[16,32,128]{2,1,0:T(8,128)(2,1)S(1)} all-to-all(bf16[16,32,128]{2,1,0:T(8,128)(2,1)S(1)} %shard_map.77), channel_id=1, replica_groups=mesh['pulse'=16,'sample'=16] {'sample'}, dimensions={0} | all-to-all | bytes 262144 | tf_op jit(solution)/shard_map/all_to_all | solution.py:356
  51.0 2.8 %shard_map.78 = (f32[8,96,128]{2,1,0:T(8,128)S(1)}, f32[8,96,128]{2,1,0:T(8,128)S(1)}) custom-call(bf16[2,512,2048]{2,1,0:T(8,128)(2,1)} %bitcast.14, bf16[512,128]{1,0:T(8,128)(2,1)S(1)} %bitcast.19), custom_call_target="tpu_custom_call" | custom-call | tf_op jit(solution)/shard_map/pallas_call | solution.py:296
  53.8 3.0 %collective-permute-start = (f32[8,96,128]{2,1,0:T(8,128)S(1)}, f32[8,96,128]{2,1,0:T(8,128)S(1)}, u32[]{:S(2)}, u32[]{:S(2)}) collective-permute-start(f32[8,96,128]{2,1,0:T(8,128)S(1)} %get-tuple-element.21), channel_id=1, source_target_pairs={{0,16},{16,0},{32,48},{48,32},{64,80},{80,64},{96,112},{112,96},{1... | collective-permute-start | bytes 1179656 | tf_op jit(solution)/shard_map/ppermute | solution.py:366
  58.3 21.9 %all_to_all.61.got_ref = f32[8,96,128]{2,1,0:T(8,128)S(1)} all-to-all(f32[8,96,128]{2,1,0:T(8,128)S(1)} %add.45), channel_id=1, replica_groups={{0,32,64,96,128,160,192,224},{16,48,80,112,144,176,208,240},{1,33,65,97..., dimensions={0} | all-to-all | bytes 786432 | tf_op jit(solution)/shard_map/all_to_all | solution.py:367
  82.4 16.7 %all_to_all.62.refs_2_.refs_3_ = bf16[16,64,128]{2,1,0:T(8,128)(2,1)S(1)} all-to-all(bf16[16,64,128]{2,1,0:T(8,128)(2,1)S(1)} %shard_map.79), channel_id=1, replica_groups=mesh['pulse'=16,'sample'=16] {'pulse'}, dimensions={0} | all-to-all | bytes 524288 | tf_op jit(solution)/shard_map/all_to_all | solution.py:370
  100.6 13.8 %all_to_all.63.got_ref = f32[16,40,128]{2,1,0:T(8,128)S(1)} all-to-all(f32[16,40,128]{2,1,0:T(8,128)S(1)} %shard_map.80), channel_id=1, replica_groups=mesh['pulse'=16,'sample'=16] {'sample'}, dimensions={0} | all-to-all | bytes 655360 | tf_op jit(solution)/shard_map/all_to_all | solution.py:376
  114.5 12.0 %all_to_all.64.refs_4_ = f32[16,8,128]{2,1,0:T(8,128)S(1)} all-to-all(f32[16,8,128]{2,1,0:T(8,128)S(1)} %broadcast_in_dim.11), channel_id=1, replica_groups=mesh['pulse'=16,'sample'=16] {'pulse'}, dimensions={0} | all-to-all | bytes 131072 | tf_op jit(solution)/shard_map/all_to_all | solution.py:380
  126.5 5.2 %shard_map.81 = (f32[16,32,128]{2,1,0:T(8,128)}, bf16[2,512,2048]{2,1,0:T(8,128)(2,1)}) custom-call(f32[8,128]{1,0:T(8,128)S(1)} %broadcast_in_dim.10.scalars.refs_0_, bf16[2,512,2048]{2,1,0:T(8,128)(2,1)S(1)} %bitcast.17, bf16[512,128]{1,0:T(8,128)(2,1)S(1)} %bitcast.21, bf16[16,64,128]{2,1,0:T(8,128)(2,1)S(1)} %all_to_all.62.refs_2_.refs_3_, ...), custom_call_target="tpu_custom_call" | custom-call | tf_op jit(solution)/shard_map/pallas_call | solution.py:296
  131.6 3.5 %all-to-all-start.6 = ((f32[16,32,128]{2,1,0:T(8,128)}), f32[16,32,128]{2,1,0:T(8,128)S(1)}, u32[]{:S(2)}, u32[]{:S(2)}) async-start(f32[16,32,128]{2,1,0:T(8,128)} %get-tuple-element.22), calls=%async_computation.6 | async-start | bytes 524288 | tf_op jit(solution)/shard_map/all_to_all | solution.py:353
  136.9 6.7 %all-to-all-done.6.got_ref = f32[16,32,128]{2,1,0:T(8,128)S(1)} async-done(((f32[16,32,128]{2,1,0:T(8,128)}), f32[16,32,128]{2,1,0:T(8,128)S(1)}, u32[]{:S(2)}, u32[]{:S(2)}) %all-to-all-start.6) | async-done | bytes 262176 | tf_op jit(solution)/shard_map/all_to_all | solution.py:353
  143.9 10.5 %all_to_all.65 = f32[16,32,128]{2,1,0:T(8,128)S(1)} all-to-all(f32[16,32,128]{2,1,0:T(8,128)S(1)} %shard_map.83), channel_id=1, replica_groups=mesh['pulse'=16,'sample'=16] {'sample'}, dimensions={0} | all-to-all | bytes 524288 | tf_op jit(solution)/shard_map/all_to_all | solution.py:356
  154.4 3.4 %shard_map.84 = (f32[8,112,128]{2,1,0:T(8,128)S(1)}, f32[8,112,128]{2,1,0:T(8,128)S(1)}) custom-call(bf16[2,512,2048]{2,1,0:T(8,128)(2,1)} %get-tuple-element.23.data_ref, bf16[512,128]{1,0:T(8,128)(2,1)S(1)} %bitcast_convert_fusion.u_ref.refs_1_.refs_2_, bf16[512,1024]{1,0:T(8,128)(2,1)} %get-tuple-element.25.refs_0_), custom_call_target="tpu_custom_call" | custom-call | tf_op jit(solution)/shard_map/pallas_call | solution.py:296
  157.8 2.3 collective-permute-start.1
  161.6 18.9 %all_to_all.66.got_ref = f32[8,112,128]{2,1,0:T(8,128)S(1)} all-to-all(f32[8,112,128]{2,1,0:T(8,128)S(1)} %add.53), channel_id=1, replica_groups={{0,32,64,96,128,160,192,224},{16,48,80,112,144,176,208,240},{1,33,65,97..., dimensions={0} | all-to-all | bytes 917504 | tf_op jit(solution)/shard_map/all_to_all | solution.py:367
  182.8 14.7 %all_to_all.67.refs_2_.v_ref.refs_3_ = bf16[16,64,128]{2,1,0:T(8,128)(2,1)S(1)} all-to-all(bf16[16,64,128]{2,1,0:T(8,128)(2,1)S(1)} %get-tuple-element.28), channel_id=1, replica_groups=mesh['pulse'=16,'sample'=16] {'pulse'}, dimensions={0} | all-to-all | bytes 524288 | tf_op jit(solution)/shard_map/all_to_all | solution.py:370
  199.4 3.5 %all-to-all-start.10 = ((f32[16,8,128]{2,1,0:T(8,128)}), f32[16,8,128]{2,1,0:T(8,128)S(1)}, u32[]{:S(2)}, u32[]{:S(2)}) async-start(f32[16,8,128]{2,1,0:T(8,128)} %shard_map.86), calls=%async_computation.10 | async-start | bytes 131072 | tf_op jit(solution)/shard_map/all_to_all | solution.py:376
  203.1 6.8 %all-to-all-done.10 = f32[16,8,128]{2,1,0:T(8,128)S(1)} async-done(((f32[16,8,128]{2,1,0:T(8,128)}), f32[16,8,128]{2,1,0:T(8,128)S(1)}, u32[]{:S(2)}, u32[]{:S(2)}) %all-to-all-start.10) | async-done | bytes 65568 | tf_op jit(solution)/shard_map/all_to_all | solution.py:376
  210.5 3.7 %all-to-all-start.11 = ((f32[16,8,128]{2,1,0:T(8,128)}), f32[16,8,128]{2,1,0:T(8,128)S(1)}, u32[]{:S(2)}, u32[]{:S(2)}) async-start(f32[16,8,128]{2,1,0:T(8,128)} %broadcast_in_dim.14), calls=%async_computation.12 | async-start | bytes 131072 | tf_op jit(solution)/shard_map/all_to_all | solution.py:380
  216.4 5.6 %all-to-all-done.11.refs_4_ = f32[16,8,128]{2,1,0:T(8,128)S(1)} async-done(((f32[16,8,128]{2,1,0:T(8,128)}), f32[16,8,128]{2,1,0:T(8,128)S(1)}, u32[]{:S(2)}, u32[]{:S(2)}) %all-to-all-start.11) | async-done | bytes 65568 | tf_op jit(solution)/shard_map/all_to_all | solution.py:380
  222.7 5.3 %shard_map.88 = bf16[2,512,2048]{2,1,0:T(8,128)(2,1)} custom-call(f32[8,128]{1,0:T(8,128)S(1)} %broadcast_in_dim.10.scalars.refs_0_, bf16[2,512,2048]{2,1,0:T(8,128)(2,1)} %bitcast.15, bf16[512,128]{1,0:T(8,128)(2,1)S(1)} %bitcast_convert_fusion.u_ref.refs_1_.refs_2_, bf16[16,64,128]{2,1,0:T(8,128)(2,1)S(1)} %all_to_all.67.refs_2_.v_ref.refs_3_, ...), custom_call_target="tpu_custom_call" | custom-call | tf_op jit(solution)/shard_map/pallas_call | solution.py:296
  (38 shorter events, 21.9 us)
Async XLA Ops:
  7.2 202.7 %reduce-scatter.2.cloned.1.call-start = ((), (), s32[]{:S(2)}) async-start(), calls=%async_computation.13 | async-start | bytes 4456448 | tf_op jit(solution)/shard_map/reduce_scatter | solution.py:342
  7.2 1.0 copy-start.2
  20.6 18.0 %all-to-all-start = ((f32[16,64,128]{2,1,0:T(8,128)}), f32[16,64,128]{2,1,0:T(8,128)S(1)}, u32[]{:S(2)}, u32[]{:S(2)}) async-start(f32[16,64,128]{2,1,0:T(8,128)} %shard_map.76), calls=%async_computation | async-start | bytes 1048576 | tf_op jit(solution)/shard_map/all_to_all | solution.py:324
  38.7 60.4 %copy-start = (bf16[1024,2048]{1,0:T(8,128)(2,1)S(1)}, bf16[1024,2048]{1,0:T(8,128)(2,1)}, u32[]{:S(2)}) copy-start(bf16[1024,2048]{1,0:T(8,128)(2,1)} %echo_ref.1) | copy-start | bytes 12582916
  53.8 4.4 %collective-permute-start = (f32[8,96,128]{2,1,0:T(8,128)S(1)}, f32[8,96,128]{2,1,0:T(8,128)S(1)}, u32[]{:S(2)}, u32[]{:S(2)}) collective-permute-start(f32[8,96,128]{2,1,0:T(8,128)S(1)} %get-tuple-element.21), channel_id=1, source_target_pairs={{0,16},{16,0},{32,48},{48,32},{64,80},{80,64},{96,112},{112,96},{1... | collective-permute-start | bytes 1179656 | tf_op jit(solution)/shard_map/ppermute | solution.py:366
  131.6 12.0 %all-to-all-start.6 = ((f32[16,32,128]{2,1,0:T(8,128)}), f32[16,32,128]{2,1,0:T(8,128)S(1)}, u32[]{:S(2)}, u32[]{:S(2)}) async-start(f32[16,32,128]{2,1,0:T(8,128)} %get-tuple-element.22), calls=%async_computation.6 | async-start | bytes 524288 | tf_op jit(solution)/shard_map/all_to_all | solution.py:353
  154.3 43.1 %copy-start.1 = (bf16[1024,2048]{1,0:T(8,128)(2,1)S(1)}, bf16[1024,2048]{1,0:T(8,128)(2,1)}, u32[]{:S(2)}) copy-start(bf16[1024,2048]{1,0:T(8,128)(2,1)} %echo_ref.1) | copy-start | bytes 12582916
  157.8 3.8 %collective-permute-start.1 = (f32[8,112,128]{2,1,0:T(8,128)S(1)}, f32[8,112,128]{2,1,0:T(8,128)S(1)}, u32[]{:S(2)}, u32[]{:S(2)}) collective-permute-start(f32[8,112,128]{2,1,0:T(8,128)S(1)} %get-tuple-element.27), channel_id=1, source_target_pairs={{0,16},{16,0},{32,48},{48,32},{64,80},{80,64},{96,112},{112,96},{1... | collective-permute-start | bytes 1376264 | tf_op jit(solution)/shard_map/ppermute | solution.py:366
  199.4 10.4 %all-to-all-start.10 = ((f32[16,8,128]{2,1,0:T(8,128)}), f32[16,8,128]{2,1,0:T(8,128)S(1)}, u32[]{:S(2)}, u32[]{:S(2)}) async-start(f32[16,8,128]{2,1,0:T(8,128)} %shard_map.86), calls=%async_computation.10 | async-start | bytes 131072 | tf_op jit(solution)/shard_map/all_to_all | solution.py:376
  210.5 11.5 %all-to-all-start.11 = ((f32[16,8,128]{2,1,0:T(8,128)}), f32[16,8,128]{2,1,0:T(8,128)S(1)}, u32[]{:S(2)}, u32[]{:S(2)}) async-start(f32[16,8,128]{2,1,0:T(8,128)} %broadcast_in_dim.14), calls=%async_computation.12 | async-start | bytes 131072 | tf_op jit(solution)/shard_map/all_to_all | solution.py:380
  215.1 0.9 copy-start.3
Sparse Core Ops, SparseCore 0:
  20.7 71.0 reduce-scatter.1

commit v2 on v1

--- a/solution.py
+++ b/solution.py
@@ -317,7 +317,8 @@
     row_blocks = pl.BlockSpec((2, bp, cols), lambda i: (0, i, 0))
     to_solve = call(
         first_products, [((16, 64, 128), F32)], echo3, sample_init.T, steps=2,
-        blocked={0: row_blocks}, blocked_out={0: pl.BlockSpec((8, 64, 128), lambda i: (i, 0, 0))},
+        blocked={0: row_blocks, 1: full((RANK, cols))},
+        blocked_out={0: pl.BlockSpec((8, 64, 128), lambda i: (i, 0, 0))},
         scratch=turned + [pltpu.VMEM((32, 128), F32)],
     )[0]
     to_solve, chirp_phase = lax.optimization_barrier((to_solve, chirp_phase))
@@ -339,9 +340,6 @@
         out_shape=[jax.ShapeDtypeStruct((2 * BINS, rows), BF16), jax.ShapeDtypeStruct((2 * BINS, cols), F32)],
         compiler_params=pltpu.CompilerParams(vmem_limit_bytes=56 * 2**20), name="doppler_products",
     )(jnp.cos(angle_a) * scale, jnp.sin(angle_a) * scale, jnp.cos(angle_b), jnp.sin(angle_b), echoes)
-    spectrum = lax.psum_scatter(
-        spectrum.reshape(groups, 2 * BINS // groups, cols), "pulse", scatter_dimension=0, tiled=True
-    )
 
     data3 = echo3
     for turn_index in range(ITERS):
@@ -373,6 +371,11 @@
             lambda *refs: residual_squares(not last, *refs), [((16, height, 128), F32)],
             echo3, u_bf, v_chunks, scratch=stacked,
         )[0]
+        if not last:
+            grams, spectrum = lax.optimization_barrier((grams, spectrum))
+            spectrum = lax.psum_scatter(
+                spectrum.reshape(groups, 2 * BINS // groups, cols), "pulse", scatter_dimension=0, tiled=True
+            )
         grams = lax.all_to_all(grams, "sample", 0, 0, tiled=True)
         sums = jnp.sum(grams[:, :8], axis=0, keepdims=True)
         if last:

time: 236 us -> 230 us (0.975)
  blocking collectives: 119 us -> 101 us
  starting transfers between devices: 23.7 us -> 28.7 us
  local copies, waits for them, and re-layouts: 5.11 us -> 8.58 us
  waiting for transfers between devices: 31.1 us -> 34.2 us
    all_to_all x2 -> x1, blocking collectives: 31.4 us -> 14.7 us  [on_device(): v_chunks = lax.all_to_all(mine[0], 'pulse', 0, 0, tiled=True)]
    all_to_all x0 -> x1, starting transfers between devices: none -> 5.04 us  [on_device(): v_chunks = lax.all_to_all(mine[0], 'pulse', 0, 0, tiled=True)]
    unnamed x10, local copies, waits for them, and re-layouts: 3.5 us -> 6.97 us
    all_to_all x0 -> x1, waiting for transfers between devices: none -> 3.23 us  [on_device(): v_chunks = lax.all_to_all(mine[0], 'pulse', 0, 0, tiled=True)]
  transfers between devices with their start and end apart: 7 -> 8, of which waited for: 6 -> 7; matrix products, arithmetic and copies ran while one was open for 1% -> 1% of each run, Pallas kernels for 10% -> 9%
where the time goes in v2:
time: 230 us; the launch traced here: 229 us
  blocking collectives  101 us (44%)
  Pallas kernels  40.1 us (17%)
  waiting for transfers between devices  34.2 us (15%)
  starting transfers between devices  28.7 us (12%)
  between operations  15.5 us (7%)
  local copies, waits for them, and re-layouts  8.58 us (4%)
    all_to_all x2, blocking collectives, on_device(): lax.all_to_all(keep, 'pulse', 0, 0, tiled=True, axis_index_groups=across_z)  40.8 us
    pallas_call x13, Pallas kernels, call(): pl.pallas_call(body, in_specs=in_specs, out_specs=out_specs, out_shape=sh...  33.6 us
    all_to_all x2, blocking collectives, on_device(): u_full = lax.all_to_all(mine, 'sample', 0, 0, tiled=True).reshape(half, 128)  20.6 us
    all_to_all x2, waiting for transfers between devices, on_device(): got = lax.all_to_all(to_solve, 'sample', 0, 0, tiled=True)  15.8 us
    all_to_all x1, blocking collectives, on_device(): v_chunks = lax.all_to_all(mine[0], 'pulse', 0, 0, tiled=True)  14.7 us
    all_to_all x1, blocking collectives, on_device(): grams = lax.all_to_all(grams, 'sample', 0, 0, tiled=True)  12.6 us
    all_to_all x1, blocking collectives, on_device(): lax.all_to_all(jnp.broadcast_to(sums, (16, 8, 128)), 'pulse', 0, 0, tiled...  12.1 us
    all_to_all x2, starting transfers between devices, on_device(): got = lax.all_to_all(to_solve, 'sample', 0, 0, tiled=True)  11.1 us
  transfers between devices with their start and end apart: 8, of which 7 were waited for; matrix products, arithmetic and copies ran while one was open for 1% of the time, Pallas kernels for 9%

profile of v2, /device:TPU:1, one launch (start us, length us, event | category | flops | bytes accessed | tf_op | source)
XLA Modules:
  0.0 229.3 jit_solution(6193290784856045312)
XLA Ops:
  7.2 4.0 %shard_map.76 = f32[16,64,128]{2,1,0:T(8,128)} custom-call(bf16[2,512,2048]{2,1,0:T(8,128)(2,1)} %bitcast.13, bf16[64,2048]{1,0:T(8,128)(2,1)} %bitcast.25), custom_call_target="tpu_custom_call" | custom-call | tf_op jit(solution)/shard_map/pallas_call | solution.py:296
  11.2 7.6 %all-to-all-start = ((f32[16,64,128]{2,1,0:T(8,128)}), f32[16,64,128]{2,1,0:T(8,128)S(1)}, u32[]{:S(2)}, u32[]{:S(2)}) async-start(f32[16,64,128]{2,1,0:T(8,128)} %shard_map.76), calls=%async_computation | async-start | bytes 1048576 | tf_op jit(solution)/shard_map/all_to_all | solution.py:325
  20.2 9.0 %all-to-all-done.got_ref = f32[16,64,128]{2,1,0:T(8,128)S(1)} async-done(((f32[16,64,128]{2,1,0:T(8,128)}), f32[16,64,128]{2,1,0:T(8,128)S(1)}, u32[]{:S(2)}, u32[]{:S(2)}) %all-to-all-start) | async-done | bytes 524320 | tf_op jit(solution)/shard_map/all_to_all | solution.py:325
  31.5 10.1 %all_to_all.60 = bf16[16,32,128]{2,1,0:T(8,128)(2,1)S(1)} all-to-all(bf16[16,32,128]{2,1,0:T(8,128)(2,1)S(1)} %shard_map.77), channel_id=1, replica_groups=mesh['pulse'=16,'sample'=16] {'sample'}, dimensions={0} | all-to-all | bytes 262144 | tf_op jit(solution)/shard_map/all_to_all | solution.py:354
  44.4 3.0 %collective-permute-start = (f32[8,96,128]{2,1,0:T(8,128)S(1)}, f32[8,96,128]{2,1,0:T(8,128)S(1)}, u32[]{:S(2)}, u32[]{:S(2)}) collective-permute-start(f32[8,96,128]{2,1,0:T(8,128)S(1)} %get-tuple-element.23), channel_id=1, source_target_pairs={{0,16},{16,0},{32,48},{48,32},{64,80},{80,64},{96,112},{112,96},{1... | collective-permute-start | bytes 1179656 | tf_op jit(solution)/shard_map/ppermute | solution.py:364
  48.8 21.9 %all_to_all.61.got_ref = f32[8,96,128]{2,1,0:T(8,128)S(1)} all-to-all(f32[8,96,128]{2,1,0:T(8,128)S(1)} %add.45), channel_id=1, replica_groups={{0,32,64,96,128,160,192,224},{16,48,80,112,144,176,208,240},{1,33,65,97..., dimensions={0} | all-to-all | bytes 786432 | tf_op jit(solution)/shard_map/all_to_all | solution.py:365
  70.7 2.9 %shard_map.79 = bf16[16,64,128]{2,1,0:T(8,128)(2,1)} custom-call(f32[8,128]{1,0:T(8,128)S(1)} %broadcast_in_dim.10.scalars.refs_0_, f32[8,96,128]{2,1,0:T(8,128)S(1)} %all_to_all.61.got_ref), custom_call_target="tpu_custom_call" | custom-call | tf_op jit(solution)/shard_map/pallas_call | solution.py:296
  73.6 5.0 %all-to-all-start.3 = ((bf16[16,64,128]{2,1,0:T(8,128)(2,1)}), bf16[16,64,128]{2,1,0:T(8,128)(2,1)S(1)}, u32[]{:S(2)}, u32[]{:S(2)}) async-start(bf16[16,64,128]{2,1,0:T(8,128)(2,1)} %shard_map.79), calls=%async_computation.3 | async-start | bytes 524288 | tf_op jit(solution)/shard_map/all_to_all | solution.py:368
  80.6 6.5 %doppler_products.1 = (bf16[512,1024]{1,0:T(8,128)(2,1)}, f32[512,2048]{1,0:T(8,128)}) custom-call(f32[16,1024]{1,0:T(8,128)} %get-tuple-element.45.ca_ref, f32[16,1024]{1,0:T(8,128)} %get-tuple-element.44.sa_ref, f32[16,1024]{1,0:T(8,128)} %get-tuple-element.47.cb_ref, f32[16,1024]{1,0:T(8,128)} %get-tuple-element.46.sb_ref, bf16[1024,2048]{1,0:T(8,128)(2,1)} %echo_ref.1), custom_call_target="tpu_custom_call" | custom-call | tf_op jit(solution)/shard_map/doppler_products/pallas_call | solution.py:336
  87.1 3.2 %all-to-all-done.3.refs_2_.refs_3_ = bf16[16,64,128]{2,1,0:T(8,128)(2,1)S(1)} async-done(((bf16[16,64,128]{2,1,0:T(8,128)(2,1)}), bf16[16,64,128]{2,1,0:T(8,128)(2,1)S(1)}, u32[]{:S(2)}, u32[]{:S(2)}) %all-to-all-start.3) | async-done | bytes 262176 | tf_op jit(solution)/shard_map/all_to_all | solution.py:368
  94.1 12.6 %all_to_all.62.got_ref = f32[16,40,128]{2,1,0:T(8,128)S(1)} all-to-all(f32[16,40,128]{2,1,0:T(8,128)S(1)} %shard_map.80), channel_id=1, replica_groups=mesh['pulse'=16,'sample'=16] {'sample'}, dimensions={0} | all-to-all | bytes 655360 | tf_op jit(solution)/shard_map/all_to_all | solution.py:379
  106.7 12.1 %all_to_all.63.refs_4_ = f32[16,8,128]{2,1,0:T(8,128)S(1)} all-to-all(f32[16,8,128]{2,1,0:T(8,128)S(1)} %broadcast_in_dim.11), channel_id=1, replica_groups=mesh['pulse'=16,'sample'=16] {'pulse'}, dimensions={0} | all-to-all | bytes 131072 | tf_op jit(solution)/shard_map/all_to_all | solution.py:383
  121.0 5.1 %shard_map.81 = (f32[16,32,128]{2,1,0:T(8,128)}, bf16[2,512,2048]{2,1,0:T(8,128)(2,1)}) custom-call(f32[8,128]{1,0:T(8,128)S(1)} %broadcast_in_dim.10.scalars.refs_0_, bf16[2,512,2048]{2,1,0:T(8,128)(2,1)S(1)} %bitcast.17, bf16[512,128]{1,0:T(8,128)(2,1)S(1)} %bitcast.21, bf16[16,64,128]{2,1,0:T(8,128)(2,1)S(1)} %all-to-all-done.3.refs_2_.refs_3_, ...), custom_call_target="tpu_custom_call" | custom-call | tf_op jit(solution)/shard_map/pallas_call | solution.py:296
  126.1 3.5 %all-to-all-start.6 = ((f32[16,32,128]{2,1,0:T(8,128)}), f32[16,32,128]{2,1,0:T(8,128)S(1)}, u32[]{:S(2)}, u32[]{:S(2)}) async-start(f32[16,32,128]{2,1,0:T(8,128)} %get-tuple-element.27), calls=%async_computation.6 | async-start | bytes 524288 | tf_op jit(solution)/shard_map/all_to_all | solution.py:351
  131.4 6.7 %all-to-all-done.6.got_ref = f32[16,32,128]{2,1,0:T(8,128)S(1)} async-done(((f32[16,32,128]{2,1,0:T(8,128)}), f32[16,32,128]{2,1,0:T(8,128)S(1)}, u32[]{:S(2)}, u32[]{:S(2)}) %all-to-all-start.6) | async-done | bytes 262176 | tf_op jit(solution)/shard_map/all_to_all | solution.py:351
  138.3 10.5 %all_to_all.64 = f32[16,32,128]{2,1,0:T(8,128)S(1)} all-to-all(f32[16,32,128]{2,1,0:T(8,128)S(1)} %shard_map.83), channel_id=1, replica_groups=mesh['pulse'=16,'sample'=16] {'sample'}, dimensions={0} | all-to-all | bytes 524288 | tf_op jit(solution)/shard_map/all_to_all | solution.py:354
  148.8 3.5 %shard_map.84 = (f32[8,112,128]{2,1,0:T(8,128)S(1)}, f32[8,112,128]{2,1,0:T(8,128)S(1)}) custom-call(bf16[2,512,2048]{2,1,0:T(8,128)(2,1)} %get-tuple-element.28.data_ref, bf16[512,128]{1,0:T(8,128)(2,1)S(1)} %bitcast_convert_fusion.u_ref.refs_1_.refs_2_, bf16[512,1024]{1,0:T(8,128)(2,1)} %get-tuple-element.29.refs_0_), custom_call_target="tpu_custom_call" | custom-call | tf_op jit(solution)/shard_map/pallas_call | solution.py:296
  156.1 18.9 %all_to_all.65.got_ref = f32[8,112,128]{2,1,0:T(8,128)S(1)} all-to-all(f32[8,112,128]{2,1,0:T(8,128)S(1)} %add.53), channel_id=1, replica_groups={{0,32,64,96,128,160,192,224},{16,48,80,112,144,176,208,240},{1,33,65,97..., dimensions={0} | all-to-all | bytes 917504 | tf_op jit(solution)/shard_map/all_to_all | solution.py:365
  177.3 14.7 %all_to_all.66.refs_2_.v_ref.refs_3_ = bf16[16,64,128]{2,1,0:T(8,128)(2,1)S(1)} all-to-all(bf16[16,64,128]{2,1,0:T(8,128)(2,1)S(1)} %get-tuple-element.32), channel_id=1, replica_groups=mesh['pulse'=16,'sample'=16] {'pulse'}, dimensions={0} | all-to-all | bytes 524288 | tf_op jit(solution)/shard_map/all_to_all | solution.py:368
  193.9 3.5 %all-to-all-start.10 = ((f32[16,8,128]{2,1,0:T(8,128)}), f32[16,8,128]{2,1,0:T(8,128)S(1)}, u32[]{:S(2)}, u32[]{:S(2)}) async-start(f32[16,8,128]{2,1,0:T(8,128)} %shard_map.86), calls=%async_computation.10 | async-start | bytes 131072 | tf_op jit(solution)/shard_map/all_to_all | solution.py:379
  197.6 6.8 %all-to-all-done.10 = f32[16,8,128]{2,1,0:T(8,128)S(1)} async-done(((f32[16,8,128]{2,1,0:T(8,128)}), f32[16,8,128]{2,1,0:T(8,128)S(1)}, u32[]{:S(2)}, u32[]{:S(2)}) %all-to-all-start.10) | async-done | bytes 65568 | tf_op jit(solution)/shard_map/all_to_all | solution.py:379
  205.0 3.7 %all-to-all-start.11 = ((f32[16,8,128]{2,1,0:T(8,128)}), f32[16,8,128]{2,1,0:T(8,128)S(1)}, u32[]{:S(2)}, u32[]{:S(2)}) async-start(f32[16,8,128]{2,1,0:T(8,128)} %broadcast_in_dim.14), calls=%async_computation.12 | async-start | bytes 131072 | tf_op jit(solution)/shard_map/all_to_all | solution.py:383
  210.9 5.6 %all-to-all-done.11.refs_4_ = f32[16,8,128]{2,1,0:T(8,128)S(1)} async-done(((f32[16,8,128]{2,1,0:T(8,128)}), f32[16,8,128]{2,1,0:T(8,128)S(1)}, u32[]{:S(2)}, u32[]{:S(2)}) %all-to-all-start.11) | async-done | bytes 65568 | tf_op jit(solution)/shard_map/all_to_all | solution.py:383
  217.2 5.2 %shard_map.88 = bf16[2,512,2048]{2,1,0:T(8,128)(2,1)} custom-call(f32[8,128]{1,0:T(8,128)S(1)} %broadcast_in_dim.10.scalars.refs_0_, bf16[2,512,2048]{2,1,0:T(8,128)(2,1)} %bitcast.15, bf16[512,128]{1,0:T(8,128)(2,1)S(1)} %bitcast_convert_fusion.u_ref.refs_1_.refs_2_, bf16[16,64,128]{2,1,0:T(8,128)(2,1)S(1)} %all_to_all.66.refs_2_.v_ref.refs_3_, ...), custom_call_target="tpu_custom_call" | custom-call | tf_op jit(solution)/shard_map/pallas_call | solution.py:296
  (39 shorter events, 28.2 us)
Async XLA Ops:
  11.2 18.0 %all-to-all-start = ((f32[16,64,128]{2,1,0:T(8,128)}), f32[16,64,128]{2,1,0:T(8,128)S(1)}, u32[]{:S(2)}, u32[]{:S(2)}) async-start(f32[16,64,128]{2,1,0:T(8,128)} %shard_map.76), calls=%async_computation | async-start | bytes 1048576 | tf_op jit(solution)/shard_map/all_to_all | solution.py:325
  44.4 4.3 %collective-permute-start = (f32[8,96,128]{2,1,0:T(8,128)S(1)}, f32[8,96,128]{2,1,0:T(8,128)S(1)}, u32[]{:S(2)}, u32[]{:S(2)}) collective-permute-start(f32[8,96,128]{2,1,0:T(8,128)S(1)} %get-tuple-element.23), channel_id=1, source_target_pairs={{0,16},{16,0},{32,48},{48,32},{64,80},{80,64},{96,112},{112,96},{1... | collective-permute-start | bytes 1179656 | tf_op jit(solution)/shard_map/ppermute | solution.py:364
  73.6 16.8 %all-to-all-start.3 = ((bf16[16,64,128]{2,1,0:T(8,128)(2,1)}), bf16[16,64,128]{2,1,0:T(8,128)(2,1)S(1)}, u32[]{:S(2)}, u32[]{:S(2)}) async-start(bf16[16,64,128]{2,1,0:T(8,128)(2,1)} %shard_map.79), calls=%async_computation.3 | async-start | bytes 524288 | tf_op jit(solution)/shard_map/all_to_all | solution.py:368
  78.6 125.8 %reduce-scatter.2.cloned.1.call-start = ((), (), s32[]{:S(2)}) async-start(), calls=%async_computation.13 | async-start | bytes 4456448 | tf_op jit(solution)/shard_map/reduce_scatter | solution.py:376
  90.4 2.2 copy-start
  118.8 2.2 copy-start.1
  126.1 12.0 %all-to-all-start.6 = ((f32[16,32,128]{2,1,0:T(8,128)}), f32[16,32,128]{2,1,0:T(8,128)S(1)}, u32[]{:S(2)}, u32[]{:S(2)}) async-start(f32[16,32,128]{2,1,0:T(8,128)} %get-tuple-element.27), calls=%async_computation.6 | async-start | bytes 524288 | tf_op jit(solution)/shard_map/all_to_all | solution.py:351
  148.8 43.1 %copy-start.2 = (bf16[1024,2048]{1,0:T(8,128)(2,1)S(1)}, bf16[1024,2048]{1,0:T(8,128)(2,1)}, u32[]{:S(2)}) copy-start(bf16[1024,2048]{1,0:T(8,128)(2,1)} %echo_ref.1) | copy-start | bytes 12582916
  152.3 3.8 %collective-permute-start.1 = (f32[8,112,128]{2,1,0:T(8,128)S(1)}, f32[8,112,128]{2,1,0:T(8,128)S(1)}, u32[]{:S(2)}, u32[]{:S(2)}) collective-permute-start(f32[8,112,128]{2,1,0:T(8,128)S(1)} %get-tuple-element.31), channel_id=1, source_target_pairs={{0,16},{16,0},{32,48},{48,32},{64,80},{80,64},{96,112},{112,96},{1... | collective-permute-start | bytes 1376264 | tf_op jit(solution)/shard_map/ppermute | solution.py:364
  193.9 10.4 %all-to-all-start.10 = ((f32[16,8,128]{2,1,0:T(8,128)}), f32[16,8,128]{2,1,0:T(8,128)S(1)}, u32[]{:S(2)}, u32[]{:S(2)}) async-start(f32[16,8,128]{2,1,0:T(8,128)} %shard_map.86), calls=%async_computation.10 | async-start | bytes 131072 | tf_op jit(solution)/shard_map/all_to_all | solution.py:379
  205.0 11.5 %all-to-all-start.11 = ((f32[16,8,128]{2,1,0:T(8,128)}), f32[16,8,128]{2,1,0:T(8,128)S(1)}, u32[]{:S(2)}, u32[]{:S(2)}) async-start(f32[16,8,128]{2,1,0:T(8,128)} %broadcast_in_dim.14), calls=%async_computation.12 | async-start | bytes 131072 | tf_op jit(solution)/shard_map/all_to_all | solution.py:383
  209.6 0.9 copy-start.3
Sparse Core Ops, SparseCore 0:
  94.2 55.4 reduce-scatter.1

commit v3 on v2

--- a/solution.py
+++ b/solution.py
@@ -8,6 +8,7 @@
 
 BINS = 256
 ITERS = 2
+FALLBACK = True
 RANK = 64
 F32 = jnp.float32
 BF16 = jnp.bfloat16
@@ -68,12 +69,13 @@
 
 
 def stack_factor(v_ref, va_ref, vb_ref, ta_ref=None, tb_ref=None):
-    chunks, rank, width = v_ref.shape
+    chunks, _, width = v_ref.shape
+    rank = RANK
     cols = chunks * width
     va_ref[rank:, :] = jnp.zeros((rank, cols), va_ref.dtype)
     vb_ref[:rank, :] = jnp.zeros((rank, cols), vb_ref.dtype)
     for j in range(chunks):
-        part = v_ref[j]
+        part = v_ref[j, :rank]
         here = slice(j * width, (j + 1) * width)
         va_ref[:rank, here] = part
         vb_ref[rank:, here] = part
@@ -105,10 +107,12 @@
     out_ref[:, 32:, :] = jnp.broadcast_to(gram[...][None], (out_ref.shape[0], 32, 128))
 
 
+def total_of(tile):
+    return jnp.sum(jnp.sum(tile, axis=0, keepdims=True), axis=1, keepdims=True)
+
+
 def level_of(sums, threshold, cells):
-    tile = jnp.sum(sums, axis=0)
-    total = jnp.sum(jnp.sum(tile, axis=0, keepdims=True), axis=1, keepdims=True)
-    return threshold * jnp.sqrt(total / cells + 1e-06)
+    return threshold * jnp.sqrt(total_of(sums) / cells + 1e-06)
 
 
 def next_products(cells, scalars, echo_ref, u_ref, v_ref, sums_ref, out_ref, clean_ref, va, vb, ta, tb, buffer, sems):
@@ -142,7 +146,7 @@
 
 
 def invert_gram(scalars, got_ref, out_ref):
-    total = jnp.sum(got_ref[:, 8:, :], axis=0)
+    total = jnp.sum(got_ref[:, 16:, :], axis=0)
     out_ref[...] = inverse_block(unpack_square(total), scalars[1:2, 0:1])
 
 
@@ -158,17 +162,52 @@
     out_ref[...] = jnp.broadcast_to(factor[None], out_ref.shape)
 
 
-def solve_samples(scalars, got_ref, out_ref, *rest):
+def solve_samples(scalars, got_ref, out_ref, rest_ref):
     total = jnp.sum(got_ref[...], axis=0)
     inverse = ridge_inverse(unpack_square(total[RANK : RANK + 32]), scalars[1:2, 0:1])
     factor = mm_exact(inverse[:, :RANK], total[:RANK]).astype(out_ref.dtype)
+    if out_ref.shape[1] > RANK:
+        inner = total_of(total[:RANK] * factor.astype(F32))
+        high = inner.astype(BF16).astype(F32)
+        middle = (inner - high).astype(BF16).astype(F32)
+        low = inner - high - middle
+        row = lax.broadcasted_iota(jnp.int32, (16, 128), 0)
+        tail = jnp.where(row == 0, high, jnp.where(row == 1, middle, jnp.where(row == 2, low, 0.0)))
+        factor = jnp.concatenate([factor, tail.astype(out_ref.dtype)], axis=0)
+        rest_ref[...] = total[RANK:]
+    else:
+        rest_ref[...] = total[RANK + 32 :]
     out_ref[...] = jnp.broadcast_to(factor[None], out_ref.shape)
-    if rest:
-        rest[0][...] = total[RANK + 32 :]
+
+
+def sample_gram(v_ref, rest_ref, out_ref):
+    chunks = v_ref.shape[0]
+    square = jnp.zeros((RANK, 128), F32)
+    inner = jnp.zeros((1, 1), F32)
+    for j in range(chunks):
+        part = v_ref[j, :RANK]
+        square = square + mm(part, jnp.concatenate([part, part], axis=0), NT)
+        tail = v_ref[j, RANK:].astype(F32)
+        inner = inner + (tail[0:1, 0:1] + (tail[1:2, 0:1] + tail[2:3, 0:1]))
+    tile = jnp.concatenate(
+        [rest_ref[32:], jnp.broadcast_to(inner, (8, 128)), pack_square(square)], axis=0
+    )
+    out_ref[...] = jnp.broadcast_to(tile[None], out_ref.shape)
+
+
+def squares_from_products(got_ref, rest_ref, sums_ref, energy_ref):
+    total = jnp.sum(got_ref[...], axis=0)
+    energy = total_of(total[:8])
+    value = energy - 2.0 * total[8:9, 0:1] + total_of(total[16:] * rest_ref[:32])
+    row = lax.broadcasted_iota(jnp.int32, (8, 128), 0)
+    lane = lax.broadcasted_iota(jnp.int32, (8, 128), 1)
+    sums_ref[...] = jnp.where((row == 0) & (lane == 0), value, 0.0)
+    energy_ref[...] = jnp.broadcast_to(energy, (8, 128))
 
 
 def sample_products(data_ref, u_ref, *refs):
-    kernel_ref = refs[0] if len(refs) == 4 else None
+    extra_ref = refs[0]
+    kernel_ref = extra_ref if extra_ref.dtype == BF16 else None
     keep_ref, send_ref, turned = refs[-3:]
     width = 128
     own = lax.axis_index("pulse") % 2 == 0
@@ -189,7 +228,11 @@
         send_ref[z, :RANK, :] = jnp.where(own, one, zero)
         keep_ref[z, RANK : RANK + 32, :] = gram
         send_ref[z, RANK : RANK + 32, :] = gram
-    if kernel_ref is not None:
+    if kernel_ref is None:
+        energy = jnp.broadcast_to(extra_ref[...][None], (chunks, 8, 128))
+        keep_ref[:, RANK + 32 :, :] = energy
+        send_ref[:, RANK + 32 :, :] = energy
+    else:
         half = kernel_ref.shape[1] // 2
         low = lanes_low((kernel_ref.shape[0], 128))
         mixed = jnp.where(
@@ -205,7 +248,7 @@
             send_ref[z, RANK + 32 :, :] = jnp.where(own, one, zero)
 
 
-def residual_squares(with_gram, echo_ref, u_ref, v_ref, out_ref, va, vb):
+def residual_squares(echo_ref, u_ref, v_ref, out_ref, va, vb):
     stack_factor(v_ref, va, vb)
     rows = u_ref.shape[0] // 2
     total = jnp.zeros((8, va.shape[1]), F32)
@@ -218,9 +261,6 @@
     tile = total[:, :128]
     for j in range(1, total.shape[1] // 128):
         tile = tile + total[:, 128 * j : 128 * (j + 1)]
-    if with_gram:
-        square = mm(va[:RANK, :], va[...] + vb[...], NT)
-        tile = jnp.concatenate([tile, pack_square(square)], axis=0)
     out_ref[...] = jnp.broadcast_to(tile[None], out_ref.shape)
 
 
@@ -259,11 +299,12 @@
         sparse_ref[h] = (residual - jnp.clip(residual, -level, level)).astype(BF16)
 
 
-def doppler_products(ca_ref, sa_ref, cb_ref, sb_ref, echo_ref, kernel_ref, out_ref):
+def doppler_products(ca_ref, sa_ref, cb_ref, sb_ref, echo_ref, kernel_ref, out_ref, energy_ref):
     groups = ca_ref.shape[0]
 
     @pl.when(pl.program_id(0) == 0)
     def _():
+        energy_ref[...] = jnp.zeros_like(energy_ref)
         cb, sb = cb_ref[...], sb_ref[...]
         for g in range(groups):
             ca, sa = ca_ref[g : g + 1, :], sa_ref[g : g + 1, :]
@@ -271,6 +312,10 @@
             kernel_ref[32 * g + 16 : 32 * (g + 1), :] = (-(sa * cb + ca * sb)).astype(BF16)
 
     out_ref[...] = mm(kernel_ref[...], echo_ref[...], NN)
+    echo = echo_ref[...].astype(F32)
+    square = jnp.sum((echo * echo).reshape(-1, 8, echo.shape[1]), axis=0)
+    for j in range(square.shape[1] // 128):
+        energy_ref[...] += square[:, 128 * j : 128 * (j + 1)]
 
 
 def full(shape):
@@ -333,11 +378,11 @@
     scale = 1.0 / jnp.sqrt(F32(pulse_total))
     table = full((16, rows))
     dcols = 512
-    kernel, spectrum = pl.pallas_call(
+    kernel, spectrum, energy = pl.pallas_call(
         doppler_products, grid=(cols // dcols,),
         in_specs=[table] * 4 + [pl.BlockSpec((rows, dcols), lambda i: (0, i))],
-        out_specs=[full((2 * BINS, rows)), pl.BlockSpec((2 * BINS, dcols), lambda i: (0, i))],
-        out_shape=[jax.ShapeDtypeStruct((2 * BINS, rows), BF16), jax.ShapeDtypeStruct((2 * BINS, cols), F32)],
+        out_specs=[full((2 * BINS, rows)), pl.BlockSpec((2 * BINS, dcols), lambda i: (0, i)), full((8, 128))],
+        out_shape=[jax.ShapeDtypeStruct((2 * BINS, rows), BF16), jax.ShapeDtypeStruct((2 * BINS, cols), F32), jax.ShapeDtypeStruct((8, 128), F32)],
         compiler_params=pltpu.CompilerParams(vmem_limit_bytes=56 * 2**20), name="doppler_products",
     )(jnp.cos(angle_a) * scale, jnp.sin(angle_a) * scale, jnp.cos(angle_b), jnp.sin(angle_b), echoes)
 
@@ -353,35 +398,50 @@
             mine = call(apply_pulses, pulse_out, got, block)[0]
         u_full = lax.all_to_all(mine, "sample", 0, 0, tiled=True).reshape(half, 128)
         u_bf = u_full.astype(BF16)
-        depth = RANK + 32 + (16 if last else 0)
-        extra = [kernel] if last else []
+        depth = RANK + 32 + (16 if last else 8)
+        extra = kernel if last else energy
         keep, send = call(
-            sample_products, [((8, depth, 128), F32)] * 2, data3, u_bf, *extra, steps=2,
-            blocked={0: pl.BlockSpec((2, half, cols // 2), lambda i: (0, 0, i)), 2: pl.BlockSpec((BINS, rows), lambda i: (i, 0))},
+            sample_products, [((8, depth, 128), F32)] * 2, data3, u_bf, extra, steps=2,
+            blocked={0: pl.BlockSpec((2, half, cols // 2), lambda i: (0, 0, i)), **({2: pl.BlockSpec((BINS, rows), lambda i: (i, 0))} if last else {})},
             blocked_out={i: pl.BlockSpec((4, depth, 128), lambda i: (i, 0, 0)) for i in range(2)},
             scratch=[pltpu.VMEM((128, half), BF16)],
         )
         keep = keep + lax.ppermute(send, "pulse", other_core)
         got = lax.all_to_all(keep, "pulse", 0, 0, tiled=True, axis_index_groups=across_z)
-        outs = [((16, RANK, 128), BF16)] + ([((16, 128), F32)] if last else [])
+        width = RANK if last else RANK + 16
+        outs = [((16, width, 128), BF16), ((16 if last else 40, 128), F32)]
         mine = call(solve_samples, outs, scalars, got)
         v_chunks = lax.all_to_all(mine[0], "pulse", 0, 0, tiled=True)
-        height = 8 if last else 40
-        grams = call(
-            lambda *refs: residual_squares(not last, *refs), [((16, height, 128), F32)],
-            echo3, u_bf, v_chunks, scratch=stacked,
-        )[0]
-        if not last:
-            grams, spectrum = lax.optimization_barrier((grams, spectrum))
+
+        def direct_squares(u_bf, v_chunks, between=lambda sums: sums):
+            sums = call(residual_squares, [((16, 8, 128), F32)], echo3, u_bf, v_chunks, scratch=stacked)[0]
+            sums = lax.all_to_all(sums, "sample", 0, 0, tiled=True)
+            sums = between(jnp.sum(sums, axis=0, keepdims=True))
+            sums = lax.all_to_all(jnp.broadcast_to(sums, (16, 8, 128)), "pulse", 0, 0, tiled=True)
+            return jnp.sum(sums, axis=0)
+
+        if last:
+            def between(sums):
+                nonlocal spectrum
+                sums, spectrum = lax.optimization_barrier((sums, spectrum))
+                return sums
+
+            sums = direct_squares(u_bf, v_chunks, between)
+        else:
+            v_chunks, spectrum = lax.optimization_barrier((v_chunks, spectrum))
             spectrum = lax.psum_scatter(
                 spectrum.reshape(groups, 2 * BINS // groups, cols), "pulse", scatter_dimension=0, tiled=True
             )
-        grams = lax.all_to_all(grams, "sample", 0, 0, tiled=True)
-        sums = jnp.sum(grams[:, :8], axis=0, keepdims=True)
-        if last:
-            sums, spectrum = lax.optimization_barrier((sums, spectrum))
-        sums = lax.all_to_all(jnp.broadcast_to(sums, (16, 8, 128)), "pulse", 0, 0, tiled=True)
-        if not last:
+            grams = call(sample_gram, [((16, 48, 128), F32)], v_chunks, mine[1])[0]
+            grams = lax.all_to_all(grams, "sample", 0, 0, tiled=True)
+            sums, total = call(squares_from_products, [((8, 128), F32)] * 2, grams, mine[1])
+            if FALLBACK:
+                sums = lax.cond(
+                    sums[0, 0] > 0.001 * total[0, 0],
+                    lambda sums, u_bf, v_chunks: sums,
+                    lambda sums, u_bf, v_chunks: direct_squares(u_bf, v_chunks),
+                    sums, u_bf, v_chunks,
+                )
             to_solve, data3 = call(
                 lambda *refs: next_products(cells, *refs),
                 [((16, 32, 128), F32), (echo3.shape, BF16)],

time: 230 us -> 226 us (0.983)
  blocking collectives: 101 us -> 83.8 us
  waiting for transfers between devices: 34.2 us -> 40.7 us
  starting transfers between devices: 28.7 us -> 33.7 us
    all_to_all x2 -> x0, blocking collectives: 24.7 us -> none  [the longest x1 12.6 us: on_device(): grams = lax.all_to_all(grams, 'sample', 0, 0, tiled=True)]
    all_to_all x1 -> x2, blocking collectives: 14.7 us -> 32.1 us  [on_device(): v_chunks = lax.all_to_all(mine[0], 'pulse', 0, 0, tiled=True)]
    all_to_all x2 -> x1, blocking collectives: 20.6 us -> 10.2 us  [on_device(): u_full = lax.all_to_all(mine, 'sample', 0, 0, tiled=True).reshape(half, 128)]
    all_to_all x1, waiting for transfers between devices: 6.77 us -> 10.6 us  [on_device(): grams = lax.all_to_all(grams, 'sample', 0, 0, tiled=True)]
    all_to_all x2 -> x3, waiting for transfers between devices: 8.82 us -> 12.3 us  [the longest x1 6.75 us: direct_squares(): sums = lax.all_to_all(sums, 'sample', 0, 0, tiled=True)]
    all_to_all x1, starting transfers between devices: 3.5 us -> 6.67 us  [on_device(): grams = lax.all_to_all(grams, 'sample', 0, 0, tiled=True)]
    all_to_all x2 -> x3, starting transfers between devices: 8.73 us -> 10.7 us  [the longest x1 3.69 us: direct_squares(): lax.all_to_all(jnp.broadcast_to(sums, (16, 8, 128)), 'pulse', 0, 0, tiled...]
    pallas_call x13 -> x14, Pallas kernels: 33.6 us -> 33.7 us  [call(): pl.pallas_call(body, in_specs=in_specs, out_specs=out_specs, out_shape=sh...]
  transfers between devices with their start and end apart: 8 -> 9, of which waited for: 7 -> 7; matrix products, arithmetic and copies ran while one was open for 1% -> 2% of each run, Pallas kernels for 9% -> 10%
where the time goes in v3:
time: 226 us; the launch traced here: 225 us
  blocking collectives  83.8 us (37%)
  waiting for transfers between devices  40.7 us (18%)
  Pallas kernels  40.1 us (18%)
  starting transfers between devices  33.7 us (15%)
  between operations  16.8 us (7%)
  local copies, waits for them, and re-layouts  8.11 us (4%)
    all_to_all x2, blocking collectives, on_device(): lax.all_to_all(keep, 'pulse', 0, 0, tiled=True, axis_index_groups=across_z)  41.5 us
    pallas_call x14, Pallas kernels, call(): pl.pallas_call(body, in_specs=in_specs, out_specs=out_specs, out_shape=sh...  33.7 us
    all_to_all x2, blocking collectives, on_device(): v_chunks = lax.all_to_all(mine[0], 'pulse', 0, 0, tiled=True)  32.1 us
    all_to_all x2, waiting for transfers between devices, on_device(): got = lax.all_to_all(to_solve, 'sample', 0, 0, tiled=True)  14.9 us
    all_to_all x2, starting transfers between devices, on_device(): got = lax.all_to_all(to_solve, 'sample', 0, 0, tiled=True)  11.1 us
    all_to_all x1, waiting for transfers between devices, on_device(): grams = lax.all_to_all(grams, 'sample', 0, 0, tiled=True)  10.6 us
    all_to_all x1, blocking collectives, on_device(): u_full = lax.all_to_all(mine, 'sample', 0, 0, tiled=True).reshape(half, 128)  10.2 us
    all_to_all x1, waiting for transfers between devices, direct_squares(): sums = lax.all_to_all(sums, 'sample', 0, 0, tiled=True)  6.75 us
  transfers between devices with their start and end apart: 9, of which 7 were waited for; matrix products, arithmetic and copies ran while one was open for 2% of the time, Pallas kernels for 10%

profile of v3, /device:TPU:1, one launch (start us, length us, event | category | flops | bytes accessed | tf_op | source)
XLA Modules:
  0.0 224.9 jit_solution(12001004543193099442)
XLA Ops:
  7.2 4.0 %shard_map.76 = f32[16,64,128]{2,1,0:T(8,128)} custom-call(bf16[2,512,2048]{2,1,0:T(8,128)(2,1)} %bitcast.14, bf16[64,2048]{1,0:T(8,128)(2,1)} %bitcast.26), custom_call_target="tpu_custom_call" | custom-call | tf_op jit(solution)/shard_map/pallas_call | solution.py:341
  11.2 7.6 %all-to-all-start.2 = ((f32[16,64,128]{2,1,0:T(8,128)}), f32[16,64,128]{2,1,0:T(8,128)S(1)}, u32[]{:S(2)}, u32[]{:S(2)}) async-start(f32[16,64,128]{2,1,0:T(8,128)} %shard_map.76), calls=%async_computation.2 | async-start | bytes 1048576 | tf_op jit(solution)/shard_map/all_to_all | solution.py:370
  20.9 8.3 %all-to-all-done.2.got_ref = f32[16,64,128]{2,1,0:T(8,128)S(1)} async-done(((f32[16,64,128]{2,1,0:T(8,128)}), f32[16,64,128]{2,1,0:T(8,128)S(1)}, u32[]{:S(2)}, u32[]{:S(2)}) %all-to-all-start.2) | async-done | bytes 524320 | tf_op jit(solution)/shard_map/all_to_all | solution.py:370
  29.3 2.9 %shard_map.77 = bf16[16,32,128]{2,1,0:T(8,128)(2,1)} custom-call(f32[8,128]{1,0:T(8,128)S(1)} %broadcast_in_dim.10.scalars.refs_0_, f32[16,64,128]{2,1,0:T(8,128)S(1)} %all-to-all-done.2.got_ref), custom_call_target="tpu_custom_call" | custom-call | tf_op jit(solution)/shard_map/pallas_call | solution.py:341
  32.2 3.5 %all-to-all-start.3 = ((bf16[16,32,128]{2,1,0:T(8,128)(2,1)}), bf16[16,32,128]{2,1,0:T(8,128)(2,1)S(1)}, u32[]{:S(2)}, u32[]{:S(2)}) async-start(bf16[16,32,128]{2,1,0:T(8,128)(2,1)} %shard_map.77), calls=%async_computation.3 | async-start | bytes 262144 | tf_op jit(solution)/shard_map/all_to_all | solution.py:399
  37.0 6.4 %doppler_products.1 = (bf16[512,1024]{1,0:T(8,128)(2,1)}, f32[512,2048]{1,0:T(8,128)}, f32[8,128]{1,0:T(8,128)}) custom-call(f32[16,1024]{1,0:T(8,128)} %get-tuple-element.71.ca_ref, f32[16,1024]{1,0:T(8,128)} %get-tuple-element.70.sa_ref, f32[16,1024]{1,0:T(8,128)} %get-tuple-element.73.cb_ref, f32[16,1024]{1,0:T(8,128)} %get-tuple-element.72.sb_ref, ...), custom_call_target="tpu_custom_call" | custom-call | tf_op jit(solution)/shard_map/doppler_products/pallas_call | solution.py:381
  44.1 2.7 %shard_map.78 = (f32[8,104,128]{2,1,0:T(8,128)S(1)}, f32[8,104,128]{2,1,0:T(8,128)S(1)}) custom-call(bf16[2,512,2048]{2,1,0:T(8,128)(2,1)} %bitcast.15, bf16[512,128]{1,0:T(8,128)(2,1)S(1)} %bitcast.20, f32[8,128]{1,0:T(8,128)S(1)} %copy-done.4), custom_call_target="tpu_custom_call" | custom-call | tf_op jit(solution)/shard_map/pallas_call | solution.py:341
  50.7 22.6 %all_to_all.65.got_ref = f32[8,104,128]{2,1,0:T(8,128)S(1)} all-to-all(f32[8,104,128]{2,1,0:T(8,128)S(1)} %add.52), channel_id=1, replica_groups={{0,32,64,96,128,160,192,224},{16,48,80,112,144,176,208,240},{1,33,65,97..., dimensions={0} | all-to-all | bytes 851968 | tf_op jit(solution)/shard_map/all_to_all | solution.py:410
  75.7 17.4 %all_to_all.66.v_ref.refs_3_ = bf16[16,80,128]{2,1,0:T(8,128)(2,1)S(1)} all-to-all(bf16[16,80,128]{2,1,0:T(8,128)(2,1)S(1)} %get-tuple-element.44), channel_id=1, replica_groups=mesh['pulse'=16,'sample'=16] {'pulse'}, dimensions={0} | all-to-all | bytes 655360 | tf_op jit(solution)/shard_map/all_to_all | solution.py:414
  94.3 6.7 %all-to-all-start.6 = ((f32[16,48,128]{2,1,0:T(8,128)}), f32[16,48,128]{2,1,0:T(8,128)S(1)}, u32[]{:S(2)}, u32[]{:S(2)}) async-start(f32[16,48,128]{2,1,0:T(8,128)} %shard_map.80), calls=%async_computation.6 | async-start | bytes 786432 | tf_op jit(solution)/shard_map/all_to_all | solution.py:436
  101.0 10.6 %all-to-all-done.6.got_ref = f32[16,48,128]{2,1,0:T(8,128)S(1)} async-done(((f32[16,48,128]{2,1,0:T(8,128)}), f32[16,48,128]{2,1,0:T(8,128)S(1)}, u32[]{:S(2)}, u32[]{:S(2)}) %all-to-all-start.6) | async-done | bytes 393248 | tf_op jit(solution)/shard_map/all_to_all | solution.py:436
  116.5 5.1 %shard_map.82 = (f32[16,32,128]{2,1,0:T(8,128)}, bf16[2,512,2048]{2,1,0:T(8,128)(2,1)}) custom-call(f32[8,128]{1,0:T(8,128)S(1)} %broadcast_in_dim.10.scalars.refs_0_, bf16[2,512,2048]{2,1,0:T(8,128)(2,1)S(1)} %bitcast.18, bf16[512,128]{1,0:T(8,128)(2,1)S(1)} %bitcast.22, bf16[16,80,128]{2,1,0:T(8,128)(2,1)S(1)} %all_to_all.66.v_ref.refs_3_, ...), custom_call_target="tpu_custom_call" | custom-call | tf_op jit(solution)/shard_map/pallas_call | solution.py:341
  121.6 3.5 %all-to-all-start.7 = ((f32[16,32,128]{2,1,0:T(8,128)}), f32[16,32,128]{2,1,0:T(8,128)S(1)}, u32[]{:S(2)}, u32[]{:S(2)}) async-start(f32[16,32,128]{2,1,0:T(8,128)} %get-tuple-element.50), calls=%async_computation.7 | async-start | bytes 524288 | tf_op jit(solution)/shard_map/all_to_all | solution.py:396
  126.9 6.6 %all-to-all-done.7.got_ref = f32[16,32,128]{2,1,0:T(8,128)S(1)} async-done(((f32[16,32,128]{2,1,0:T(8,128)}), f32[16,32,128]{2,1,0:T(8,128)S(1)}, u32[]{:S(2)}, u32[]{:S(2)}) %all-to-all-start.7) | async-done | bytes 262176 | tf_op jit(solution)/shard_map/all_to_all | solution.py:396
  133.7 10.2 %all_to_all.67 = f32[16,32,128]{2,1,0:T(8,128)S(1)} all-to-all(f32[16,32,128]{2,1,0:T(8,128)S(1)} %shard_map.84), channel_id=1, replica_groups=mesh['pulse'=16,'sample'=16] {'sample'}, dimensions={0} | all-to-all | bytes 524288 | tf_op jit(solution)/shard_map/all_to_all | solution.py:399
  143.9 3.4 %shard_map.85 = (f32[8,112,128]{2,1,0:T(8,128)S(1)}, f32[8,112,128]{2,1,0:T(8,128)S(1)}) custom-call(bf16[2,512,2048]{2,1,0:T(8,128)(2,1)} %get-tuple-element.51.data_ref, bf16[512,128]{1,0:T(8,128)(2,1)S(1)} %bitcast_convert_fusion.u_ref.refs_2_, bf16[512,1024]{1,0:T(8,128)(2,1)} %get-tuple-element.52.refs_0_), custom_call_target="tpu_custom_call" | custom-call | tf_op jit(solution)/shard_map/pallas_call | solution.py:341
  147.4 2.8 %collective-permute-start.1 = (f32[8,112,128]{2,1,0:T(8,128)S(1)}, f32[8,112,128]{2,1,0:T(8,128)S(1)}, u32[]{:S(2)}, u32[]{:S(2)}) collective-permute-start(f32[8,112,128]{2,1,0:T(8,128)S(1)} %get-tuple-element.54), channel_id=1, source_target_pairs={{0,16},{16,0},{32,48},{48,32},{64,80},{80,64},{96,112},{112,96},{1... | collective-permute-start | bytes 1376264 | tf_op jit(solution)/shard_map/ppermute | solution.py:409
  151.7 18.9 %all_to_all.68.got_ref = f32[8,112,128]{2,1,0:T(8,128)S(1)} all-to-all(f32[8,112,128]{2,1,0:T(8,128)S(1)} %add.53), channel_id=1, replica_groups={{0,32,64,96,128,160,192,224},{16,48,80,112,144,176,208,240},{1,33,65,97..., dimensions={0} | all-to-all | bytes 917504 | tf_op jit(solution)/shard_map/all_to_all | solution.py:410
  172.8 14.7 %all_to_all.69.v_ref.refs_3_ = bf16[16,64,128]{2,1,0:T(8,128)(2,1)S(1)} all-to-all(bf16[16,64,128]{2,1,0:T(8,128)(2,1)S(1)} %get-tuple-element.55), channel_id=1, replica_groups=mesh['pulse'=16,'sample'=16] {'pulse'}, dimensions={0} | all-to-all | bytes 524288 | tf_op jit(solution)/shard_map/all_to_all | solution.py:414
  189.5 3.5 %all-to-all-start.11 = ((f32[16,8,128]{2,1,0:T(8,128)}), f32[16,8,128]{2,1,0:T(8,128)S(1)}, u32[]{:S(2)}, u32[]{:S(2)}) async-start(f32[16,8,128]{2,1,0:T(8,128)} %shard_map.87), calls=%async_computation.11 | async-start | bytes 131072 | tf_op jit(solution)/shard_map/all_to_all | solution.py:418
  193.1 6.8 %all-to-all-done.11 = f32[16,8,128]{2,1,0:T(8,128)S(1)} async-done(((f32[16,8,128]{2,1,0:T(8,128)}), f32[16,8,128]{2,1,0:T(8,128)S(1)}, u32[]{:S(2)}, u32[]{:S(2)}) %all-to-all-start.11) | async-done | bytes 65568 | tf_op jit(solution)/shard_map/all_to_all | solution.py:418
  200.5 3.7 %all-to-all-start.12 = ((f32[16,8,128]{2,1,0:T(8,128)}), f32[16,8,128]{2,1,0:T(8,128)S(1)}, u32[]{:S(2)}, u32[]{:S(2)}) async-start(f32[16,8,128]{2,1,0:T(8,128)} %broadcast_in_dim.17), calls=%async_computation.13 | async-start | bytes 131072 | tf_op jit(solution)/shard_map/all_to_all | solution.py:420
  206.5 5.6 %all-to-all-done.12 = f32[16,8,128]{2,1,0:T(8,128)S(1)} async-done(((f32[16,8,128]{2,1,0:T(8,128)}), f32[16,8,128]{2,1,0:T(8,128)S(1)}, u32[]{:S(2)}, u32[]{:S(2)}) %all-to-all-start.12) | async-done | bytes 65568 | tf_op jit(solution)/shard_map/all_to_all | solution.py:420
  212.8 5.2 %shard_map.89 = bf16[2,512,2048]{2,1,0:T(8,128)(2,1)} custom-call(f32[8,128]{1,0:T(8,128)S(1)} %broadcast_in_dim.10.scalars.refs_0_, bf16[2,512,2048]{2,1,0:T(8,128)(2,1)} %bitcast.17, bf16[512,128]{1,0:T(8,128)(2,1)S(1)} %bitcast_convert_fusion.u_ref.refs_2_, bf16[16,64,128]{2,1,0:T(8,128)(2,1)S(1)} %all_to_all.69.v_ref.refs_3_, ...), custom_call_target="tpu_custom_call" | custom-call | tf_op jit(solution)/shard_map/pallas_call | solution.py:341
  (42 shorter events, 25.3 us)
Async XLA Ops:
  11.2 18.0 %all-to-all-start.2 = ((f32[16,64,128]{2,1,0:T(8,128)}), f32[16,64,128]{2,1,0:T(8,128)S(1)}, u32[]{:S(2)}, u32[]{:S(2)}) async-start(f32[16,64,128]{2,1,0:T(8,128)} %shard_map.76), calls=%async_computation.2 | async-start | bytes 1048576 | tf_op jit(solution)/shard_map/all_to_all | solution.py:370
  32.2 11.3 %all-to-all-start.3 = ((bf16[16,32,128]{2,1,0:T(8,128)(2,1)}), bf16[16,32,128]{2,1,0:T(8,128)(2,1)S(1)}, u32[]{:S(2)}, u32[]{:S(2)}) async-start(bf16[16,32,128]{2,1,0:T(8,128)(2,1)} %shard_map.77), calls=%async_computation.3 | async-start | bytes 262144 | tf_op jit(solution)/shard_map/all_to_all | solution.py:399
  35.7 164.2 %reduce-scatter.2.cloned.1.call-start = ((), (), s32[]{:S(2)}) async-start(), calls=%async_computation.14 | async-start | bytes 4456448 | tf_op jit(solution)/shard_map/reduce_scatter | solution.py:432
  43.4 0.7 copy-start.4
  46.9 3.7 %collective-permute-start = (f32[8,104,128]{2,1,0:T(8,128)S(1)}, f32[8,104,128]{2,1,0:T(8,128)S(1)}, u32[]{:S(2)}, u32[]{:S(2)}) collective-permute-start(f32[8,104,128]{2,1,0:T(8,128)S(1)} %get-tuple-element.43), channel_id=1, source_target_pairs={{0,16},{16,0},{32,48},{48,32},{64,80},{80,64},{96,112},{112,96},{1... | collective-permute-start | bytes 1277960 | tf_op jit(solution)/shard_map/ppermute | solution.py:409
  94.3 17.2 %all-to-all-start.6 = ((f32[16,48,128]{2,1,0:T(8,128)}), f32[16,48,128]{2,1,0:T(8,128)S(1)}, u32[]{:S(2)}, u32[]{:S(2)}) async-start(f32[16,48,128]{2,1,0:T(8,128)} %shard_map.80), calls=%async_computation.6 | async-start | bytes 786432 | tf_op jit(solution)/shard_map/all_to_all | solution.py:436
  114.3 2.3 %copy-start = (bf16[1024,2048]{1,0:T(8,128)(2,1)S(1)}, bf16[1024,2048]{1,0:T(8,128)(2,1)}, u32[]{:S(2)}) copy-start(bf16[1024,2048]{1,0:T(8,128)(2,1)} %echo_ref.1) | copy-start | bytes 12582916
  121.6 11.9 %all-to-all-start.7 = ((f32[16,32,128]{2,1,0:T(8,128)}), f32[16,32,128]{2,1,0:T(8,128)S(1)}, u32[]{:S(2)}, u32[]{:S(2)}) async-start(f32[16,32,128]{2,1,0:T(8,128)} %get-tuple-element.50), calls=%async_computation.7 | async-start | bytes 524288 | tf_op jit(solution)/shard_map/all_to_all | solution.py:396
  143.9 43.6 %copy-start.1 = (bf16[1024,2048]{1,0:T(8,128)(2,1)S(1)}, bf16[1024,2048]{1,0:T(8,128)(2,1)}, u32[]{:S(2)}) copy-start(bf16[1024,2048]{1,0:T(8,128)(2,1)} %echo_ref.1) | copy-start | bytes 12582916
  147.4 4.3 %collective-permute-start.1 = (f32[8,112,128]{2,1,0:T(8,128)S(1)}, f32[8,112,128]{2,1,0:T(8,128)S(1)}, u32[]{:S(2)}, u32[]{:S(2)}) collective-permute-start(f32[8,112,128]{2,1,0:T(8,128)S(1)} %get-tuple-element.54), channel_id=1, source_target_pairs={{0,16},{16,0},{32,48},{48,32},{64,80},{80,64},{96,112},{112,96},{1... | collective-permute-start | bytes 1376264 | tf_op jit(solution)/shard_map/ppermute | solution.py:409
  189.5 10.4 %all-to-all-start.11 = ((f32[16,8,128]{2,1,0:T(8,128)}), f32[16,8,128]{2,1,0:T(8,128)S(1)}, u32[]{:S(2)}, u32[]{:S(2)}) async-start(f32[16,8,128]{2,1,0:T(8,128)} %shard_map.87), calls=%async_computation.11 | async-start | bytes 131072 | tf_op jit(solution)/shard_map/all_to_all | solution.py:418
  200.5 11.5 %all-to-all-start.12 = ((f32[16,8,128]{2,1,0:T(8,128)}), f32[16,8,128]{2,1,0:T(8,128)S(1)}, u32[]{:S(2)}, u32[]{:S(2)}) async-start(f32[16,8,128]{2,1,0:T(8,128)} %broadcast_in_dim.17), calls=%async_computation.13 | async-start | bytes 131072 | tf_op jit(solution)/shard_map/all_to_all | solution.py:420
  205.2 0.9 copy-start.3
Sparse Core Ops, SparseCore 0:
  93.2 57.3 reduce-scatter.1

commit v4 on v3

--- a/solution.py
+++ b/solution.py
@@ -264,7 +264,35 @@
     out_ref[...] = jnp.broadcast_to(tile[None], out_ref.shape)
 
 
-def correct_doppler(v_ref, dop_ref, ku_ref, dop_out):
+def add_parts(*refs):
+    count = len(refs) - 6
+    a_ref, b_ref = refs[:2]
+    outs, (a_buf, b_buf, in_sems, out_sems) = refs[2 : 2 + count], refs[2 + count :]
+    own = lax.axis_index("pulse") // 2
+    loads = []
+    for k in range(count):
+        chunk = (own + k) % count
+        pair = (
+            pltpu.make_async_copy(a_ref.at[chunk], a_buf.at[k], in_sems.at[0, k]),
+            pltpu.make_async_copy(b_ref.at[chunk], b_buf.at[k], in_sems.at[1, k]),
+        )
+        for copy in pair:
+            copy.start()
+        loads.append(pair)
+    stores = []
+    for k in range(count):
+        for copy in loads[k]:
+            copy.wait()
+        a_buf[k] = a_buf[k] + b_buf[k]
+        copy = pltpu.make_async_copy(a_buf.at[k], outs[k], out_sems.at[k])
+        copy.start()
+        stores.append(copy)
+    for copy in stores:
+        copy.wait()
+
+
+def correct_doppler(v_ref, ku_ref, *refs):
+    dop_refs, dop_out = refs[:-1], refs[-1]
     ku = ku_ref[...]
     high = ku.astype(BF16)
     rest = ku - high.astype(F32)
@@ -280,7 +308,10 @@
         here = slice(j * width, (j + 1) * width)
         fix = mm(parts, v_ref[j], NN)
         fix = fix[:32] + (fix[32:64] + fix[64:])
-        value = dop_ref[0, :, here] - fix
+        value = dop_refs[0][:, here]
+        for dop_ref in dop_refs[1:]:
+            value = value + dop_ref[:, here]
+        value = value - fix
         dop_out[:, 0, here] = value[:16]
         dop_out[:, 1, here] = value[16:]
 
@@ -299,7 +330,7 @@
         sparse_ref[h] = (residual - jnp.clip(residual, -level, level)).astype(BF16)
 
 
-def doppler_products(ca_ref, sa_ref, cb_ref, sb_ref, echo_ref, kernel_ref, out_ref, energy_ref):
+def doppler_products(ca_ref, sa_ref, cb_ref, sb_ref, echo_ref, kernel_ref, keep_ref, send_ref, energy_ref):
     groups = ca_ref.shape[0]
 
     @pl.when(pl.program_id(0) == 0)
@@ -311,7 +342,12 @@
             kernel_ref[32 * g : 32 * g + 16, :] = (ca * cb - sa * sb).astype(BF16)
             kernel_ref[32 * g + 16 : 32 * (g + 1), :] = (-(sa * cb + ca * sb)).astype(BF16)
 
-    out_ref[...] = mm(kernel_ref[...], echo_ref[...], NN)
+    own = lax.axis_index("pulse") % 2 == 0
+    product = mm(kernel_ref[...], echo_ref[...], NN)
+    for z in range(keep_ref.shape[0]):
+        zero, one = product[64 * z : 64 * z + 32], product[64 * z + 32 : 64 * z + 64]
+        keep_ref[z] = jnp.where(own, zero, one)
+        send_ref[z] = jnp.where(own, one, zero)
     echo = echo_ref[...].astype(F32)
     square = jnp.sum((echo * echo).reshape(-1, 8, echo.shape[1]), axis=0)
     for j in range(square.shape[1] // 128):
@@ -378,14 +414,16 @@
     scale = 1.0 / jnp.sqrt(F32(pulse_total))
     table = full((16, rows))
     dcols = 512
-    kernel, spectrum, energy = pl.pallas_call(
+    kernel, spectrum, spectrum_sent, energy = pl.pallas_call(
         doppler_products, grid=(cols // dcols,),
         in_specs=[table] * 4 + [pl.BlockSpec((rows, dcols), lambda i: (0, i))],
-        out_specs=[full((2 * BINS, rows)), pl.BlockSpec((2 * BINS, dcols), lambda i: (0, i)), full((8, 128))],
-        out_shape=[jax.ShapeDtypeStruct((2 * BINS, rows), BF16), jax.ShapeDtypeStruct((2 * BINS, cols), F32), jax.ShapeDtypeStruct((8, 128), F32)],
+        out_specs=[full((2 * BINS, rows)), *[pl.BlockSpec((groups // 2, 32, dcols), lambda i: (0, 0, i))] * 2, full((8, 128))],
+        out_shape=[jax.ShapeDtypeStruct((2 * BINS, rows), BF16), *[jax.ShapeDtypeStruct((groups // 2, 32, cols), F32)] * 2, jax.ShapeDtypeStruct((8, 128), F32)],
         compiler_params=pltpu.CompilerParams(vmem_limit_bytes=56 * 2**20), name="doppler_products",
     )(jnp.cos(angle_a) * scale, jnp.sin(angle_a) * scale, jnp.cos(angle_b), jnp.sin(angle_b), echoes)
 
+    spectrum_got = lax.ppermute(spectrum_sent, "pulse", other_core)
+    ring = groups // 2
     data3 = echo3
     for turn_index in range(ITERS):
         last = turn_index == ITERS - 1
@@ -428,12 +466,20 @@
 
             sums = direct_squares(u_bf, v_chunks, between)
         else:
-            v_chunks, spectrum = lax.optimization_barrier((v_chunks, spectrum))
-            spectrum = lax.psum_scatter(
-                spectrum.reshape(groups, 2 * BINS // groups, cols), "pulse", scatter_dimension=0, tiled=True
-            )
             grams = call(sample_gram, [((16, 48, 128), F32)], v_chunks, mine[1])[0]
             grams = lax.all_to_all(grams, "sample", 0, 0, tiled=True)
+            pieces = pl.pallas_call(
+                add_parts, in_specs=[HBM] * 2, out_specs=[HBM] * ring,
+                out_shape=[pltpu.HBM(spectrum.shape[1:], F32)] * ring, name="add_parts",
+                scratch_shapes=[pltpu.VMEM(spectrum.shape, F32)] * 2
+                + [pltpu.SemaphoreType.DMA((2, ring)), pltpu.SemaphoreType.DMA((ring,))],
+                compiler_params=pltpu.CompilerParams(vmem_limit_bytes=28 * 2**20),
+            )(spectrum, spectrum_got)
+            spectrum = [pieces[0]]
+            for step in range(1, ring):
+                spectrum.append(
+                    lax.ppermute(pieces[step], "pulse", [(i, (i + 2 * step) % groups) for i in range(groups)])
+                )
             sums, total = call(squares_from_products, [((8, 128), F32)] * 2, grams, mine[1])
             if FALLBACK:
                 sums = lax.cond(
@@ -448,7 +494,7 @@
                 scalars, echo3, u_bf, v_chunks, sums, in_hbm=(1,),
                 scratch=stacked + turned + [pltpu.VMEM((2, 2, bp, cols), BF16), pltpu.SemaphoreType.DMA((2, 2))],
             )
-    doppler = call(correct_doppler, [((16, 2, cols), F32)], v_chunks, spectrum, mine[1])[0]
+    doppler = call(correct_doppler, [((16, 2, cols), F32)], v_chunks, mine[1], *spectrum)[0]
     sums, doppler = lax.optimization_barrier((sums, doppler))
     sparse = call(
         lambda *refs: finish(cells, *refs), [(echo3.shape, BF16)],

time: 226 us -> 250 us (1.11)
  waiting for transfers between devices: 40.7 us -> 63.2 us
  starting transfers between devices: 33.7 us -> 56 us
  blocking collectives: 83.8 us -> 69.1 us
  between operations: 16.8 us -> 3.42 us
  Pallas kernels: 40.1 us -> 43.5 us
    ppermute x0 -> x8, waiting for transfers between devices: none -> 24.1 us  [the longest x7 24.1 us: on_device(): lax.ppermute(pieces[step], 'pulse', [(i, (i + 2 * step) % groups) for i i...]
    ppermute x0 -> x8, starting transfers between devices: none -> 16.8 us  [the longest x7 16.3 us: on_device(): lax.ppermute(pieces[step], 'pulse', [(i, (i + 2 * step) % groups) for i i...]
    all_to_all x2 -> x1, blocking collectives: 32.1 us -> 17.4 us  [on_device(): v_chunks = lax.all_to_all(mine[0], 'pulse', 0, 0, tiled=True)]
    all_to_all x0 -> x1, starting transfers between devices: none -> 3.83 us  [on_device(): v_chunks = lax.all_to_all(mine[0], 'pulse', 0, 0, tiled=True)]
    pallas_call x0 -> x1, Pallas kernels: none -> 2.57 us  [on_device(): pl.pallas_call(add_parts, in_specs=[HBM] * 2, out_specs=[HBM] * ring, out...]
    unnamed x10 -> x12, local copies, waits for them, and re-layouts: 5.48 us -> 6.64 us
  transfers between devices with their start and end apart: 9 -> 17, of which waited for: 7 -> 13; matrix products, arithmetic and copies ran while one was open for 2% -> 2% of each run, Pallas kernels for 10% -> 8%
where the time goes in v4:
time: 250 us; the launch traced here: 249 us
  blocking collectives  69.1 us (28%)
  waiting for transfers between devices  63.2 us (25%)
  starting transfers between devices  56 us (22%)
  Pallas kernels  43.5 us (17%)
  local copies, waits for them, and re-layouts  9.99 us (4%)
  between operations  3.42 us (1%)
  other arithmetic  3.25 us (1%)
    all_to_all x2, blocking collectives, on_device(): lax.all_to_all(keep, 'pulse', 0, 0, tiled=True, axis_index_groups=across_z)  41.5 us
    pallas_call x14, Pallas kernels, call(): pl.pallas_call(body, in_specs=in_specs, out_specs=out_specs, out_shape=sh...  34.5 us
    ppermute x7, waiting for transfers between devices, on_device(): lax.ppermute(pieces[step], 'pulse', [(i, (i + 2 * step) % groups) for i i...  24.1 us
    all_to_all x1, blocking collectives, on_device(): v_chunks = lax.all_to_all(mine[0], 'pulse', 0, 0, tiled=True)  17.4 us
    ppermute x7, starting transfers between devices, on_device(): lax.ppermute(pieces[step], 'pulse', [(i, (i + 2 * step) % groups) for i i...  16.3 us
    all_to_all x2, waiting for transfers between devices, on_device(): got = lax.all_to_all(to_solve, 'sample', 0, 0, tiled=True)  14.5 us
    all_to_all x2, starting transfers between devices, on_device(): got = lax.all_to_all(to_solve, 'sample', 0, 0, tiled=True)  11.1 us
    all_to_all x1, waiting for transfers between devices, on_device(): grams = lax.all_to_all(grams, 'sample', 0, 0, tiled=True)  10.6 us
  transfers between devices with their start and end apart: 17, of which 13 were waited for; matrix products, arithmetic and copies ran while one was open for 2% of the time, Pallas kernels for 8%

profile of v4, /device:TPU:1, one launch (start us, length us, event | category | flops | bytes accessed | tf_op | source)
XLA Modules:
  0.0 248.7 jit_solution(9739562177388328013)
XLA Ops:
  0.6 4.0 %shard_map.76 = f32[16,64,128]{2,1,0:T(8,128)} custom-call(bf16[2,512,2048]{2,1,0:T(8,128)(2,1)} %bitcast.13, bf16[64,2048]{1,0:T(8,128)(2,1)} %bitcast.24), custom_call_target="tpu_custom_call" | custom-call | tf_op jit(solution)/shard_map/pallas_call | solution.py:377
  4.7 7.6 %all-to-all-start.2 = ((f32[16,64,128]{2,1,0:T(8,128)}), f32[16,64,128]{2,1,0:T(8,128)S(1)}, u32[]{:S(2)}, u32[]{:S(2)}) async-start(f32[16,64,128]{2,1,0:T(8,128)} %shard_map.76), calls=%async_computation.2 | async-start | bytes 1048576 | tf_op jit(solution)/shard_map/all_to_all | solution.py:406
  14.3 8.3 %all-to-all-done.2.got_ref = f32[16,64,128]{2,1,0:T(8,128)S(1)} async-done(((f32[16,64,128]{2,1,0:T(8,128)}), f32[16,64,128]{2,1,0:T(8,128)S(1)}, u32[]{:S(2)}, u32[]{:S(2)}) %all-to-all-start.2) | async-done | bytes 524320 | tf_op jit(solution)/shard_map/all_to_all | solution.py:406
  25.6 3.5 %all-to-all-start.3 = ((bf16[16,32,128]{2,1,0:T(8,128)(2,1)}), bf16[16,32,128]{2,1,0:T(8,128)(2,1)S(1)}, u32[]{:S(2)}, u32[]{:S(2)}) async-start(bf16[16,32,128]{2,1,0:T(8,128)(2,1)} %shard_map.77), calls=%async_computation.3 | async-start | bytes 262144 | tf_op jit(solution)/shard_map/all_to_all | solution.py:437
  30.4 6.5 %doppler_products.1 = (bf16[512,1024]{1,0:T(8,128)(2,1)}, f32[8,32,2048]{2,1,0:T(8,128)}, f32[8,32,2048]{2,1,0:T(8,128)}, f32[8,128]{1,0:T(8,128)}) custom-call(f32[16,1024]{1,0:T(8,128)} %get-tuple-element.99.ca_ref, f32[16,1024]{1,0:T(8,128)} %get-tuple-element.98.sa_ref, f32[16,1024]{1,0:T(8,128)} %get-tuple-element.101.cb_ref, ...), custom_call_target="tpu_custom_call" | custom-call | tf_op jit(solution)/shard_map/doppler_products/pallas_call | solution.py:417
  44.1 22.6 %all_to_all.65.got_ref = f32[8,104,128]{2,1,0:T(8,128)S(1)} all-to-all(f32[8,104,128]{2,1,0:T(8,128)S(1)} %add.50), channel_id=1, replica_groups={{0,32,64,96,128,160,192,224},{16,48,80,112,144,176,208,240},{1,33,65,97..., dimensions={0} | all-to-all | bytes 851968 | tf_op jit(solution)/shard_map/all_to_all | solution.py:448
  69.1 17.4 %all_to_all.66.v_ref.refs_3_ = bf16[16,80,128]{2,1,0:T(8,128)(2,1)S(1)} all-to-all(bf16[16,80,128]{2,1,0:T(8,128)(2,1)S(1)} %get-tuple-element.58), channel_id=1, replica_groups=mesh['pulse'=16,'sample'=16] {'pulse'}, dimensions={0} | all-to-all | bytes 655360 | tf_op jit(solution)/shard_map/all_to_all | solution.py:452
  87.8 6.7 %all-to-all-start.6 = ((f32[16,48,128]{2,1,0:T(8,128)}), f32[16,48,128]{2,1,0:T(8,128)S(1)}, u32[]{:S(2)}, u32[]{:S(2)}) async-start(f32[16,48,128]{2,1,0:T(8,128)} %shard_map.80), calls=%async_computation.6 | async-start | bytes 786432 | tf_op jit(solution)/shard_map/all_to_all | solution.py:470
  94.5 10.6 %all-to-all-done.6.got_ref = f32[16,48,128]{2,1,0:T(8,128)S(1)} async-done(((f32[16,48,128]{2,1,0:T(8,128)}), f32[16,48,128]{2,1,0:T(8,128)S(1)}, u32[]{:S(2)}, u32[]{:S(2)}) %all-to-all-start.6) | async-done | bytes 393248 | tf_op jit(solution)/shard_map/all_to_all | solution.py:470
  109.9 5.1 %shard_map.82 = (f32[16,32,128]{2,1,0:T(8,128)}, bf16[2,512,2048]{2,1,0:T(8,128)(2,1)}) custom-call(f32[8,128]{1,0:T(8,128)S(1)} %broadcast_in_dim.10.scalars.refs_0_, bf16[2,512,2048]{2,1,0:T(8,128)(2,1)S(1)} %bitcast.17, bf16[512,128]{1,0:T(8,128)(2,1)S(1)} %bitcast.21, bf16[16,80,128]{2,1,0:T(8,128)(2,1)S(1)} %all_to_all.66.v_ref.refs_3_, ...), custom_call_target="tpu_custom_call" | custom-call | tf_op jit(solution)/shard_map/pallas_call | solution.py:377
  115.0 3.5 %all-to-all-start.7 = ((f32[16,32,128]{2,1,0:T(8,128)}), f32[16,32,128]{2,1,0:T(8,128)S(1)}, u32[]{:S(2)}, u32[]{:S(2)}) async-start(f32[16,32,128]{2,1,0:T(8,128)} %get-tuple-element.62), calls=%async_computation.7 | async-start | bytes 524288 | tf_op jit(solution)/shard_map/all_to_all | solution.py:434
  120.8 6.1 %all-to-all-done.7.got_ref = f32[16,32,128]{2,1,0:T(8,128)S(1)} async-done(((f32[16,32,128]{2,1,0:T(8,128)}), f32[16,32,128]{2,1,0:T(8,128)S(1)}, u32[]{:S(2)}, u32[]{:S(2)}) %all-to-all-start.7) | async-done | bytes 262176 | tf_op jit(solution)/shard_map/all_to_all | solution.py:434
  127.1 10.2 %all_to_all.67 = f32[16,32,128]{2,1,0:T(8,128)S(1)} all-to-all(f32[16,32,128]{2,1,0:T(8,128)S(1)} %shard_map.84), channel_id=1, replica_groups=mesh['pulse'=16,'sample'=16] {'sample'}, dimensions={0} | all-to-all | bytes 524288 | tf_op jit(solution)/shard_map/all_to_all | solution.py:437
  137.3 3.4 %shard_map.85 = (f32[8,112,128]{2,1,0:T(8,128)S(1)}, f32[8,112,128]{2,1,0:T(8,128)S(1)}) custom-call(bf16[2,512,2048]{2,1,0:T(8,128)(2,1)} %get-tuple-element.63.data_ref, bf16[512,128]{1,0:T(8,128)(2,1)S(1)} %bitcast_convert_fusion.u_ref.refs_2_, bf16[512,1024]{1,0:T(8,128)(2,1)} %get-tuple-element.64.refs_0_), custom_call_target="tpu_custom_call" | custom-call | tf_op jit(solution)/shard_map/pallas_call | solution.py:377
  145.0 18.9 %all_to_all.68.got_ref = f32[8,112,128]{2,1,0:T(8,128)S(1)} all-to-all(f32[8,112,128]{2,1,0:T(8,128)S(1)} %add.51), channel_id=1, replica_groups={{0,32,64,96,128,160,192,224},{16,48,80,112,144,176,208,240},{1,33,65,97..., dimensions={0} | all-to-all | bytes 917504 | tf_op jit(solution)/shard_map/all_to_all | solution.py:448
  166.9 3.8 %all-to-all-start.10 = ((bf16[16,64,128]{2,1,0:T(8,128)(2,1)}), bf16[16,64,128]{2,1,0:T(8,128)(2,1)S(1)}, u32[]{:S(2)}, u32[]{:S(2)}) async-start(bf16[16,64,128]{2,1,0:T(8,128)(2,1)} %get-tuple-element.67), calls=%async_computation.10 | async-start | bytes 524288 | tf_op jit(solution)/shard_map/all_to_all | solution.py:452
  187.6 7.3 %collective-permute-done.4.refs_2_ = f32[32,2048]{1,0:T(8,128)S(1)} collective-permute-done((f32[32,2048]{1,0:T(8,128)}, f32[32,2048]{1,0:T(8,128)S(1)}, u32[]{:S(2)}, u32[]{:S(2)}) %collective-permute-start.4) | collective-permute-done | bytes 262176 | tf_op jit(solution)/shard_map/ppermute | solution.py:481
  194.9 3.7 %collective-permute-start.9 = (f32[32,2048]{1,0:T(8,128)}, f32[32,2048]{1,0:T(8,128)S(1)}, u32[]{:S(2)}, u32[]{:S(2)}) collective-permute-start(f32[32,2048]{1,0:T(8,128)} %get-tuple-element.77), channel_id=1, source_target_pairs={{0,224},{16,240},{32,0},{48,16},{64,32},{80,48},{96,64},{112,80},{... | collective-permute-start | bytes 786440 | tf_op jit(solution)/shard_map/ppermute | solution.py:481
  202.9 3.5 %all-to-all-start.11 = ((f32[16,8,128]{2,1,0:T(8,128)}), f32[16,8,128]{2,1,0:T(8,128)S(1)}, u32[]{:S(2)}, u32[]{:S(2)}) async-start(f32[16,8,128]{2,1,0:T(8,128)} %shard_map.87), calls=%async_computation.11 | async-start | bytes 131072 | tf_op jit(solution)/shard_map/all_to_all | solution.py:456
  207.2 5.6 %all-to-all-done.11 = f32[16,8,128]{2,1,0:T(8,128)S(1)} async-done(((f32[16,8,128]{2,1,0:T(8,128)}), f32[16,8,128]{2,1,0:T(8,128)S(1)}, u32[]{:S(2)}, u32[]{:S(2)}) %all-to-all-start.11) | async-done | bytes 65568 | tf_op jit(solution)/shard_map/all_to_all | solution.py:456
  213.5 10.2 %collective-permute-done.6.refs_4_ = f32[32,2048]{1,0:T(8,128)S(1)} collective-permute-done((f32[32,2048]{1,0:T(8,128)}, f32[32,2048]{1,0:T(8,128)S(1)}, u32[]{:S(2)}, u32[]{:S(2)}) %collective-permute-start.6) | collective-permute-done | bytes 262176 | tf_op jit(solution)/shard_map/ppermute | solution.py:481
  228.5 5.4 %all-to-all-start.12 = ((f32[16,8,128]{2,1,0:T(8,128)}), f32[16,8,128]{2,1,0:T(8,128)}, u32[]{:S(2)}, u32[]{:S(2)}) async-start(f32[16,8,128]{2,1,0:T(8,128)} %broadcast_in_dim.17), calls=%async_computation.12 | async-start | bytes 131072 | tf_op jit(solution)/shard_map/all_to_all | solution.py:458
  236.2 5.6 %all-to-all-done.12 = f32[16,8,128]{2,1,0:T(8,128)} async-done(((f32[16,8,128]{2,1,0:T(8,128)}), f32[16,8,128]{2,1,0:T(8,128)}, u32[]{:S(2)}, u32[]{:S(2)}) %all-to-all-start.12) | async-done | bytes 65568 | tf_op jit(solution)/shard_map/all_to_all | solution.py:458
  243.4 5.3 %shard_map.89 = bf16[2,512,2048]{2,1,0:T(8,128)(2,1)} custom-call(f32[8,128]{1,0:T(8,128)S(1)} %broadcast_in_dim.10.scalars.refs_0_, bf16[2,512,2048]{2,1,0:T(8,128)(2,1)} %bitcast.16, bf16[512,128]{1,0:T(8,128)(2,1)S(1)} %bitcast_convert_fusion.u_ref.refs_2_, bf16[16,64,128]{2,1,0:T(8,128)(2,1)S(1)} %all-to-all-done.10.v_ref.refs_3_, ...), custom_call_target="tpu_custom_call" | custom-call | tf_op jit(solution)/shard_map/pallas_call | solution.py:377
  (59 shorter events, 60.3 us)
Async XLA Ops:
  4.7 18.0 %all-to-all-start.2 = ((f32[16,64,128]{2,1,0:T(8,128)}), f32[16,64,128]{2,1,0:T(8,128)S(1)}, u32[]{:S(2)}, u32[]{:S(2)}) async-start(f32[16,64,128]{2,1,0:T(8,128)} %shard_map.76), calls=%async_computation.2 | async-start | bytes 1048576 | tf_op jit(solution)/shard_map/all_to_all | solution.py:406
  25.6 11.3 %all-to-all-start.3 = ((bf16[16,32,128]{2,1,0:T(8,128)(2,1)}), bf16[16,32,128]{2,1,0:T(8,128)(2,1)S(1)}, u32[]{:S(2)}, u32[]{:S(2)}) async-start(bf16[16,32,128]{2,1,0:T(8,128)(2,1)} %shard_map.77), calls=%async_computation.3 | async-start | bytes 262144 | tf_op jit(solution)/shard_map/all_to_all | solution.py:437
  36.9 0.7 copy-start.5
  40.3 3.8 %collective-permute-start = (f32[8,104,128]{2,1,0:T(8,128)S(1)}, f32[8,104,128]{2,1,0:T(8,128)S(1)}, u32[]{:S(2)}, u32[]{:S(2)}) collective-permute-start(f32[8,104,128]{2,1,0:T(8,128)S(1)} %get-tuple-element.57), channel_id=1, source_target_pairs={{0,16},{16,0},{32,48},{48,32},{64,80},{80,64},{96,112},{112,96},{1... | collective-permute-start | bytes 1277960 | tf_op jit(solution)/shard_map/ppermute | solution.py:447
  87.8 17.2 %all-to-all-start.6 = ((f32[16,48,128]{2,1,0:T(8,128)}), f32[16,48,128]{2,1,0:T(8,128)S(1)}, u32[]{:S(2)}, u32[]{:S(2)}) async-start(f32[16,48,128]{2,1,0:T(8,128)} %shard_map.80), calls=%async_computation.6 | async-start | bytes 786432 | tf_op jit(solution)/shard_map/all_to_all | solution.py:470
  107.7 2.2 copy-start
  115.0 11.9 %all-to-all-start.7 = ((f32[16,32,128]{2,1,0:T(8,128)}), f32[16,32,128]{2,1,0:T(8,128)S(1)}, u32[]{:S(2)}, u32[]{:S(2)}) async-start(f32[16,32,128]{2,1,0:T(8,128)} %get-tuple-element.62), calls=%async_computation.7 | async-start | bytes 524288 | tf_op jit(solution)/shard_map/all_to_all | solution.py:434
  118.6 52.1 %collective-permute-start.2 = (f32[8,32,2048]{2,1,0:T(8,128)}, f32[8,32,2048]{2,1,0:T(8,128)}, u32[]{:S(2)}, u32[]{:S(2)}) collective-permute-start(f32[8,32,2048]{2,1,0:T(8,128)} %get-tuple-element.69), channel_id=1, source_target_pairs={{0,16},{16,0},{32,48},{48,32},{64,80},{80,64},{96,112},{112,96},{1... | collective-permute-start | bytes 6291464 | tf_op jit(solution)/shard_map/ppermute | solution.py:425
  137.3 33.4 %copy-start.3 = (f32[8,32,2048]{2,1,0:T(8,128)S(1)}, f32[8,32,2048]{2,1,0:T(8,128)}, u32[]{:S(2)}) copy-start(f32[8,32,2048]{2,1,0:T(8,128)} %get-tuple-element.68.refs_0_) | copy-start | bytes 6291460
  140.7 4.2 %collective-permute-start.1 = (f32[8,112,128]{2,1,0:T(8,128)S(1)}, f32[8,112,128]{2,1,0:T(8,128)S(1)}, u32[]{:S(2)}, u32[]{:S(2)}) collective-permute-start(f32[8,112,128]{2,1,0:T(8,128)S(1)} %get-tuple-element.66), channel_id=1, source_target_pairs={{0,16},{16,0},{32,48},{48,32},{64,80},{80,64},{96,112},{112,96},{1... | collective-permute-start | bytes 1376264 | tf_op jit(solution)/shard_map/ppermute | solution.py:447
  166.9 31.8 %all-to-all-start.10 = ((bf16[16,64,128]{2,1,0:T(8,128)(2,1)}), bf16[16,64,128]{2,1,0:T(8,128)(2,1)S(1)}, u32[]{:S(2)}, u32[]{:S(2)}) async-start(bf16[16,64,128]{2,1,0:T(8,128)(2,1)} %get-tuple-element.67), calls=%async_computation.10 | async-start | bytes 524288 | tf_op jit(solution)/shard_map/all_to_all | solution.py:452
  173.3 12.2 %collective-permute-start.3 = (f32[32,2048]{1,0:T(8,128)}, f32[32,2048]{1,0:T(8,128)S(1)}, u32[]{:S(2)}, u32[]{:S(2)}) collective-permute-start(f32[32,2048]{1,0:T(8,128)} %get-tuple-element.71), channel_id=1, source_target_pairs={{0,32},{16,48},{32,64},{48,80},{64,96},{80,112},{96,128},{112,144}... | collective-permute-start | bytes 786440 | tf_op jit(solution)/shard_map/ppermute | solution.py:481
  174.7 20.2 %collective-permute-start.4 = (f32[32,2048]{1,0:T(8,128)}, f32[32,2048]{1,0:T(8,128)S(1)}, u32[]{:S(2)}, u32[]{:S(2)}) collective-permute-start(f32[32,2048]{1,0:T(8,128)} %get-tuple-element.72), channel_id=1, source_target_pairs={{0,64},{16,80},{32,96},{48,112},{64,128},{80,144},{96,160},{112,17... | collective-permute-start | bytes 786440 | tf_op jit(solution)/shard_map/ppermute | solution.py:481
  176.8 36.7 %collective-permute-start.5 = (f32[32,2048]{1,0:T(8,128)}, f32[32,2048]{1,0:T(8,128)S(1)}, u32[]{:S(2)}, u32[]{:S(2)}) collective-permute-start(f32[32,2048]{1,0:T(8,128)} %get-tuple-element.73), channel_id=1, source_target_pairs={{0,96},{16,112},{32,128},{48,144},{64,160},{80,176},{96,192},{112,... | collective-permute-start | bytes 786440 | tf_op jit(solution)/shard_map/ppermute | solution.py:481
  179.3 44.5 %collective-permute-start.6 = (f32[32,2048]{1,0:T(8,128)}, f32[32,2048]{1,0:T(8,128)S(1)}, u32[]{:S(2)}, u32[]{:S(2)}) collective-permute-start(f32[32,2048]{1,0:T(8,128)} %get-tuple-element.74), channel_id=1, source_target_pairs={{0,128},{16,144},{32,160},{48,176},{64,192},{80,208},{96,224},{112... | collective-permute-start | bytes 786440 | tf_op jit(solution)/shard_map/ppermute | solution.py:481
  181.3 42.5 %collective-permute-start.7 = (f32[32,2048]{1,0:T(8,128)}, f32[32,2048]{1,0:T(8,128)S(1)}, u32[]{:S(2)}, u32[]{:S(2)}) collective-permute-start(f32[32,2048]{1,0:T(8,128)} %get-tuple-element.75), channel_id=1, source_target_pairs={{0,160},{16,176},{32,192},{48,208},{64,224},{80,240},{96,0},{112,1... | collective-permute-start | bytes 786440 | tf_op jit(solution)/shard_map/ppermute | solution.py:481
  185.5 39.4 %collective-permute-start.8 = (f32[32,2048]{1,0:T(8,128)}, f32[32,2048]{1,0:T(8,128)S(1)}, u32[]{:S(2)}, u32[]{:S(2)}) collective-permute-start(f32[32,2048]{1,0:T(8,128)} %get-tuple-element.76), channel_id=1, source_target_pairs={{0,192},{16,208},{32,224},{48,240},{64,0},{80,16},{96,32},{112,48}... | collective-permute-start | bytes 786440 | tf_op jit(solution)/shard_map/ppermute | solution.py:481
  194.9 33.0 %collective-permute-start.9 = (f32[32,2048]{1,0:T(8,128)}, f32[32,2048]{1,0:T(8,128)S(1)}, u32[]{:S(2)}, u32[]{:S(2)}) collective-permute-start(f32[32,2048]{1,0:T(8,128)} %get-tuple-element.77), channel_id=1, source_target_pairs={{0,224},{16,240},{32,0},{48,16},{64,32},{80,48},{96,64},{112,80},{... | collective-permute-start | bytes 786440 | tf_op jit(solution)/shard_map/ppermute | solution.py:481
  198.7 2.2 copy-start.1
  200.9 35.0 %copy-start.4 = (f32[32,2048]{1,0:T(8,128)S(1)}, f32[32,2048]{1,0:T(8,128)}, u32[]{:S(2)}) copy-start(f32[32,2048]{1,0:T(8,128)} %get-tuple-element.80.refs_0_) | copy-start | bytes 786436
  202.9 10.0 %all-to-all-start.11 = ((f32[16,8,128]{2,1,0:T(8,128)}), f32[16,8,128]{2,1,0:T(8,128)S(1)}, u32[]{:S(2)}, u32[]{:S(2)}) async-start(f32[16,8,128]{2,1,0:T(8,128)} %shard_map.87), calls=%async_computation.11 | async-start | bytes 131072 | tf_op jit(solution)/shard_map/all_to_all | solution.py:456
  228.5 13.3 %all-to-all-start.12 = ((f32[16,8,128]{2,1,0:T(8,128)}), f32[16,8,128]{2,1,0:T(8,128)}, u32[]{:S(2)}, u32[]{:S(2)}) async-start(f32[16,8,128]{2,1,0:T(8,128)} %broadcast_in_dim.17), calls=%async_computation.12 | async-start | bytes 131072 | tf_op jit(solution)/shard_map/all_to_all | solution.py:458

commit v5 on v4

--- a/solution.py
+++ b/solution.py
@@ -115,26 +115,39 @@
     return threshold * jnp.sqrt(total_of(sums) / cells + 1e-06)
 
 
+def start_loads(echo_ref, buffer, sems):
+    loads = {}
+    rows = buffer.shape[2]
+    for i in range(buffer.shape[1]):
+        for h in range(2):
+            copy = pltpu.make_async_copy(echo_ref.at[h, pl.ds(i * rows, rows)], buffer.at[h, i], sems.at[0, h, i])
+            copy.start()
+            loads[h, i] = copy
+    return loads
+
+
 def next_products(cells, scalars, echo_ref, u_ref, v_ref, sums_ref, out_ref, clean_ref, va, vb, ta, tb, buffer, sems):
+    loads = start_loads(echo_ref, buffer, sems)
     stack_factor(v_ref, va, vb, ta, tb)
+    level = level_of(sums_ref[...], scalars[0:1, 0:1], cells)
+    rows = buffer.shape[2]
     copies = []
-    level = level_of(sums_ref[...], scalars[0:1, 0:1], cells)
-    rows = u_ref.shape[0] // 2
-    for i in range(2):
+    for i in range(buffer.shape[1]):
         here = slice(i * rows, (i + 1) * rows)
         part = None
         for h, stacked, turned in ((0, va, ta), (1, vb, tb)):
-            echo = echo_ref[h, here].astype(F32)
+            loads[h, i].wait()
+            echo = buffer[h, i].astype(F32)
             residual = echo - mm(u_ref[here], stacked[...], NN)
             sparse = residual - jnp.clip(residual, -level, level)
             cleaned = (echo - sparse).astype(BF16)
             buffer[h, i] = cleaned
-            copy = pltpu.make_async_copy(buffer.at[h, i], clean_ref.at[h, pl.ds(i * rows, rows)], sems.at[h, i])
+            copy = pltpu.make_async_copy(buffer.at[h, i], clean_ref.at[h, pl.ds(i * rows, rows)], sems.at[1, h, i])
             copy.start()
             copies.append(copy)
             term = mm(cleaned, turned[...], NN)
             part = term if part is None else part + term
-        out_ref[8 * i : 8 * (i + 1)] = part.reshape(8, 32, 128)
+        out_ref[(rows // 32) * i : (rows // 32) * (i + 1)] = part.reshape(rows // 32, 32, 128)
     for copy in copies:
         copy.wait()
 
@@ -195,14 +208,14 @@
     out_ref[...] = jnp.broadcast_to(tile[None], out_ref.shape)
 
 
-def squares_from_products(got_ref, rest_ref, sums_ref, energy_ref):
+def squares_from_products(got_ref, rest_ref, sums_ref, safe_ref):
     total = jnp.sum(got_ref[...], axis=0)
     energy = total_of(total[:8])
     value = energy - 2.0 * total[8:9, 0:1] + total_of(total[16:] * rest_ref[:32])
     row = lax.broadcasted_iota(jnp.int32, (8, 128), 0)
     lane = lax.broadcasted_iota(jnp.int32, (8, 128), 1)
     sums_ref[...] = jnp.where((row == 0) & (lane == 0), value, 0.0)
-    energy_ref[...] = jnp.broadcast_to(energy, (8, 128))
+    safe_ref[...] = jnp.broadcast_to(jnp.where(value > 0.001 * energy, 1.0, 0.0), (8, 128))
 
 
 def sample_products(data_ref, u_ref, *refs):
@@ -292,7 +305,7 @@
 
 
 def correct_doppler(v_ref, ku_ref, *refs):
-    dop_refs, dop_out = refs[:-1], refs[-1]
+    dop_refs, (out_ref, dop_out, sems) = refs[:-3], refs[-3:]
     ku = ku_ref[...]
     high = ku.astype(BF16)
     rest = ku - high.astype(F32)
@@ -314,20 +327,28 @@
         value = value - fix
         dop_out[:, 0, here] = value[:16]
         dop_out[:, 1, here] = value[16:]
-
-
-def finish(cells, scalars, echo_ref, u_ref, v_ref, sums_ref, sparse_ref, va, vb, level_ref):
-    @pl.when(pl.program_id(0) == 0)
-    def _():
-        stack_factor(v_ref, va, vb)
-        level_ref[...] = jnp.broadcast_to(level_of(sums_ref[...], scalars[0:1, 0:1], cells), (1, 128))
-
-    level = level_ref[0:1, 0:1]
-    rows = echo_ref.shape[1]
-    u = u_ref[pl.ds(pl.multiple_of(pl.program_id(0) * rows, rows), rows), :]
-    for h, stacked in ((0, va), (1, vb)):
-        residual = echo_ref[h].astype(F32) - mm(u, stacked[...], NN)
-        sparse_ref[h] = (residual - jnp.clip(residual, -level, level)).astype(BF16)
+    copy = pltpu.make_async_copy(dop_out, out_ref, sems.at[0])
+    copy.start()
+    copy.wait()
+
+
+def finish(cells, scalars, echo_ref, u_ref, v_ref, sums_ref, sparse_ref, va, vb, buffer, sems):
+    loads = start_loads(echo_ref, buffer, sems)
+    stack_factor(v_ref, va, vb)
+    level = level_of(sums_ref[...], scalars[0:1, 0:1], cells)
+    rows = buffer.shape[2]
+    copies = []
+    for i in range(buffer.shape[1]):
+        here = slice(i * rows, (i + 1) * rows)
+        for h, stacked in ((0, va), (1, vb)):
+            loads[h, i].wait()
+            residual = buffer[h, i].astype(F32) - mm(u_ref[here], stacked[...], NN)
+            buffer[h, i] = (residual - jnp.clip(residual, -level, level)).astype(BF16)
+            copy = pltpu.make_async_copy(buffer.at[h, i], sparse_ref.at[h, pl.ds(i * rows, rows)], sems.at[1, h, i])
+            copy.start()
+            copies.append(copy)
+    for copy in copies:
+        copy.wait()
 
 
 def doppler_products(ca_ref, sa_ref, cb_ref, sb_ref, echo_ref, kernel_ref, keep_ref, send_ref, energy_ref):
@@ -395,6 +416,7 @@
     turned = [pltpu.VMEM((cols, 128), BF16)] * 2
 
     bp = half // 2
+    block_buffer = [pltpu.VMEM((2, 2, bp, cols), BF16), pltpu.SemaphoreType.DMA((2, 2, 2))]
     row_blocks = pl.BlockSpec((2, bp, cols), lambda i: (0, i, 0))
     to_solve = call(
         first_products, [((16, 64, 128), F32)], echo3, sample_init.T, steps=2,
@@ -480,10 +502,10 @@
                 spectrum.append(
                     lax.ppermute(pieces[step], "pulse", [(i, (i + 2 * step) % groups) for i in range(groups)])
                 )
-            sums, total = call(squares_from_products, [((8, 128), F32)] * 2, grams, mine[1])
+            sums, safe = call(squares_from_products, [((8, 128), F32)] * 2, grams, mine[1])
             if FALLBACK:
                 sums = lax.cond(
-                    sums[0, 0] > 0.001 * total[0, 0],
+                    safe[0, 0] > 0.5,
                     lambda sums, u_bf, v_chunks: sums,
                     lambda sums, u_bf, v_chunks: direct_squares(u_bf, v_chunks),
                     sums, u_bf, v_chunks,
@@ -491,15 +513,17 @@
             to_solve, data3 = call(
                 lambda *refs: next_products(cells, *refs),
                 [((16, 32, 128), F32), (echo3.shape, BF16)],
-                scalars, echo3, u_bf, v_chunks, sums, in_hbm=(1,),
-                scratch=stacked + turned + [pltpu.VMEM((2, 2, bp, cols), BF16), pltpu.SemaphoreType.DMA((2, 2))],
+                scalars, echo3, u_bf, v_chunks, sums, blocked={1: HBM}, in_hbm=(1,),
+                scratch=stacked + turned + block_buffer,
             )
-    doppler = call(correct_doppler, [((16, 2, cols), F32)], v_chunks, mine[1], *spectrum)[0]
+    doppler = call(
+        correct_doppler, [((16, 2, cols), F32)], v_chunks, mine[1], *spectrum, in_hbm=(0,),
+        scratch=[pltpu.VMEM((16, 2, cols), F32), pltpu.SemaphoreType.DMA((1,))],
+    )[0]
     sums, doppler = lax.optimization_barrier((sums, doppler))
     sparse = call(
         lambda *refs: finish(cells, *refs), [(echo3.shape, BF16)],
-        scalars, echo3, u_bf, v_chunks, sums, steps=2, blocked={1: row_blocks}, blocked_out={0: row_blocks},
-        scratch=stacked + [pltpu.VMEM((1, 128), F32)],
+        scalars, echo3, u_bf, v_chunks, sums, blocked={1: HBM}, in_hbm=(0,), scratch=stacked + block_buffer,
     )[0]
     turned_factor = u_full.T
     pulse_factor = jnp.concatenate([turned_factor[:RANK], turned_factor[RANK:]], axis=1).T

time: 250 us -> 247 us (0.988)
  local copies, waits for them, and re-layouts: 9.99 us -> 5.87 us
    unnamed x12 -> x9, local copies, waits for them, and re-layouts: 6.64 us -> 3.75 us
  transfers between devices with their start and end apart: 17 -> 17, of which waited for: 13 -> 13; matrix products, arithmetic and copies ran while one was open for 2% -> 1% of each run, Pallas kernels for 8% -> 8%
where the time goes in v5:
time: 247 us; the launch traced here: 245 us
  blocking collectives  69.1 us (28%)
  waiting for transfers between devices  64.2 us (26%)
  starting transfers between devices  56 us (23%)
  Pallas kernels  44.8 us (18%)
  local copies, waits for them, and re-layouts  5.87 us (2%)
  between operations  2.95 us (1%)
    all_to_all x2, blocking collectives, on_device(): lax.all_to_all(keep, 'pulse', 0, 0, tiled=True, axis_index_groups=across_z)  41.5 us
    pallas_call x14, Pallas kernels, call(): pl.pallas_call(body, in_specs=in_specs, out_specs=out_specs, out_shape=sh...  35.8 us
    ppermute x7, waiting for transfers between devices, on_device(): lax.ppermute(pieces[step], 'pulse', [(i, (i + 2 * step) % groups) for i i...  24.2 us
    all_to_all x1, blocking collectives, on_device(): v_chunks = lax.all_to_all(mine[0], 'pulse', 0, 0, tiled=True)  17.4 us
    ppermute x7, starting transfers between devices, on_device(): lax.ppermute(pieces[step], 'pulse', [(i, (i + 2 * step) % groups) for i i...  16.3 us
    all_to_all x2, waiting for transfers between devices, on_device(): got = lax.all_to_all(to_solve, 'sample', 0, 0, tiled=True)  14.4 us
    all_to_all x2, starting transfers between devices, on_device(): got = lax.all_to_all(to_solve, 'sample', 0, 0, tiled=True)  11.1 us
    all_to_all x1, waiting for transfers between devices, on_device(): grams = lax.all_to_all(grams, 'sample', 0, 0, tiled=True)  10.6 us
  transfers between devices with their start and end apart: 17, of which 13 were waited for; matrix products, arithmetic and copies ran while one was open for 1% of the time, Pallas kernels for 8%

profile of v5, /device:TPU:1, one launch (start us, length us, event | category | flops | bytes accessed | tf_op | source)
XLA Modules:
  0.0 245.4 jit_solution(7793682951975629398)
XLA Ops:
  0.6 4.0 %shard_map.76 = f32[16,64,128]{2,1,0:T(8,128)} custom-call(bf16[2,512,2048]{2,1,0:T(8,128)(2,1)} %bitcast.13, bf16[64,2048]{1,0:T(8,128)(2,1)} %bitcast.24), custom_call_target="tpu_custom_call" | custom-call | tf_op jit(solution)/shard_map/pallas_call | solution.py:398
  4.7 7.6 %all-to-all-start.2 = ((f32[16,64,128]{2,1,0:T(8,128)}), f32[16,64,128]{2,1,0:T(8,128)S(1)}, u32[]{:S(2)}, u32[]{:S(2)}) async-start(f32[16,64,128]{2,1,0:T(8,128)} %shard_map.76), calls=%async_computation.2 | async-start | bytes 1048576 | tf_op jit(solution)/shard_map/all_to_all | solution.py:428
  14.3 8.3 %all-to-all-done.2.got_ref = f32[16,64,128]{2,1,0:T(8,128)S(1)} async-done(((f32[16,64,128]{2,1,0:T(8,128)}), f32[16,64,128]{2,1,0:T(8,128)S(1)}, u32[]{:S(2)}, u32[]{:S(2)}) %all-to-all-start.2) | async-done | bytes 524320 | tf_op jit(solution)/shard_map/all_to_all | solution.py:428
  25.6 3.5 %all-to-all-start.3 = ((bf16[16,32,128]{2,1,0:T(8,128)(2,1)}), bf16[16,32,128]{2,1,0:T(8,128)(2,1)S(1)}, u32[]{:S(2)}, u32[]{:S(2)}) async-start(bf16[16,32,128]{2,1,0:T(8,128)(2,1)} %shard_map.77), calls=%async_computation.3 | async-start | bytes 262144 | tf_op jit(solution)/shard_map/all_to_all | solution.py:459
  30.4 6.5 %doppler_products.1 = (bf16[512,1024]{1,0:T(8,128)(2,1)}, f32[8,32,2048]{2,1,0:T(8,128)}, f32[8,32,2048]{2,1,0:T(8,128)}, f32[8,128]{1,0:T(8,128)}) custom-call(f32[16,1024]{1,0:T(8,128)} %get-tuple-element.99.ca_ref, f32[16,1024]{1,0:T(8,128)} %get-tuple-element.98.sa_ref, f32[16,1024]{1,0:T(8,128)} %get-tuple-element.101.cb_ref, ...), custom_call_target="tpu_custom_call" | custom-call | tf_op jit(solution)/shard_map/doppler_products/pallas_call | solution.py:439
  44.1 22.6 %all_to_all.65.got_ref = f32[8,104,128]{2,1,0:T(8,128)S(1)} all-to-all(f32[8,104,128]{2,1,0:T(8,128)S(1)} %add.50), channel_id=1, replica_groups={{0,32,64,96,128,160,192,224},{16,48,80,112,144,176,208,240},{1,33,65,97..., dimensions={0} | all-to-all | bytes 851968 | tf_op jit(solution)/shard_map/all_to_all | solution.py:470
  69.1 17.4 %all_to_all.66.v_ref.refs_3_ = bf16[16,80,128]{2,1,0:T(8,128)(2,1)S(1)} all-to-all(bf16[16,80,128]{2,1,0:T(8,128)(2,1)S(1)} %get-tuple-element.58), channel_id=1, replica_groups=mesh['pulse'=16,'sample'=16] {'pulse'}, dimensions={0} | all-to-all | bytes 655360 | tf_op jit(solution)/shard_map/all_to_all | solution.py:474
  87.8 6.7 %all-to-all-start.6 = ((f32[16,48,128]{2,1,0:T(8,128)}), f32[16,48,128]{2,1,0:T(8,128)S(1)}, u32[]{:S(2)}, u32[]{:S(2)}) async-start(f32[16,48,128]{2,1,0:T(8,128)} %shard_map.80), calls=%async_computation.6 | async-start | bytes 786432 | tf_op jit(solution)/shard_map/all_to_all | solution.py:492
  94.4 10.6 %all-to-all-done.6.got_ref = f32[16,48,128]{2,1,0:T(8,128)S(1)} async-done(((f32[16,48,128]{2,1,0:T(8,128)}), f32[16,48,128]{2,1,0:T(8,128)S(1)}, u32[]{:S(2)}, u32[]{:S(2)}) %all-to-all-start.6) | async-done | bytes 393248 | tf_op jit(solution)/shard_map/all_to_all | solution.py:492
  106.5 6.6 %shard_map.82 = (f32[16,32,128]{2,1,0:T(8,128)}, bf16[2,512,2048]{2,1,0:T(8,128)(2,1)}) custom-call(f32[8,128]{1,0:T(8,128)S(1)} %broadcast_in_dim.10.scalars.refs_0_, bf16[2,512,2048]{2,1,0:T(8,128)(2,1)} %bitcast.16, bf16[512,128]{1,0:T(8,128)(2,1)S(1)} %bitcast.21, bf16[16,80,128]{2,1,0:T(8,128)(2,1)S(1)} %all_to_all.66.v_ref.refs_3_, ...), custom_call_target="tpu_custom_call" | custom-call | tf_op jit(solution)/shard_map/pallas_call | solution.py:398
  113.2 3.5 %all-to-all-start.7 = ((f32[16,32,128]{2,1,0:T(8,128)}), f32[16,32,128]{2,1,0:T(8,128)S(1)}, u32[]{:S(2)}, u32[]{:S(2)}) async-start(f32[16,32,128]{2,1,0:T(8,128)} %get-tuple-element.62), calls=%async_computation.7 | async-start | bytes 524288 | tf_op jit(solution)/shard_map/all_to_all | solution.py:456
  118.9 6.1 %all-to-all-done.7.got_ref = f32[16,32,128]{2,1,0:T(8,128)S(1)} async-done(((f32[16,32,128]{2,1,0:T(8,128)}), f32[16,32,128]{2,1,0:T(8,128)S(1)}, u32[]{:S(2)}, u32[]{:S(2)}) %all-to-all-start.7) | async-done | bytes 262176 | tf_op jit(solution)/shard_map/all_to_all | solution.py:456
  125.2 10.2 %all_to_all.67 = f32[16,32,128]{2,1,0:T(8,128)S(1)} all-to-all(f32[16,32,128]{2,1,0:T(8,128)S(1)} %shard_map.84), channel_id=1, replica_groups=mesh['pulse'=16,'sample'=16] {'sample'}, dimensions={0} | all-to-all | bytes 524288 | tf_op jit(solution)/shard_map/all_to_all | solution.py:459
  135.4 3.4 %shard_map.85 = (f32[8,112,128]{2,1,0:T(8,128)S(1)}, f32[8,112,128]{2,1,0:T(8,128)S(1)}) custom-call(bf16[2,512,2048]{2,1,0:T(8,128)(2,1)} %get-tuple-element.63.data_ref, bf16[512,128]{1,0:T(8,128)(2,1)S(1)} %bitcast_convert_fusion.u_ref.refs_2_, bf16[512,1024]{1,0:T(8,128)(2,1)} %get-tuple-element.64.refs_0_), custom_call_target="tpu_custom_call" | custom-call | tf_op jit(solution)/shard_map/pallas_call | solution.py:398
  143.1 18.9 %all_to_all.68.got_ref = f32[8,112,128]{2,1,0:T(8,128)S(1)} all-to-all(f32[8,112,128]{2,1,0:T(8,128)S(1)} %add.51), channel_id=1, replica_groups={{0,32,64,96,128,160,192,224},{16,48,80,112,144,176,208,240},{1,33,65,97..., dimensions={0} | all-to-all | bytes 917504 | tf_op jit(solution)/shard_map/all_to_all | solution.py:470
  165.0 3.8 %all-to-all-start.10 = ((bf16[16,64,128]{2,1,0:T(8,128)(2,1)}), bf16[16,64,128]{2,1,0:T(8,128)(2,1)S(1)}, u32[]{:S(2)}, u32[]{:S(2)}) async-start(bf16[16,64,128]{2,1,0:T(8,128)(2,1)} %get-tuple-element.67), calls=%async_computation.10 | async-start | bytes 524288 | tf_op jit(solution)/shard_map/all_to_all | solution.py:474
  185.7 7.3 %collective-permute-done.4.refs_2_ = f32[32,2048]{1,0:T(8,128)S(1)} collective-permute-done((f32[32,2048]{1,0:T(8,128)}, f32[32,2048]{1,0:T(8,128)S(1)}, u32[]{:S(2)}, u32[]{:S(2)}) %collective-permute-start.4) | collective-permute-done | bytes 262176 | tf_op jit(solution)/shard_map/ppermute | solution.py:503
  193.1 3.7 %collective-permute-start.9 = (f32[32,2048]{1,0:T(8,128)}, f32[32,2048]{1,0:T(8,128)S(1)}, u32[]{:S(2)}, u32[]{:S(2)}) collective-permute-start(f32[32,2048]{1,0:T(8,128)} %get-tuple-element.77), channel_id=1, source_target_pairs={{0,224},{16,240},{32,0},{48,16},{64,32},{80,48},{96,64},{112,80},{... | collective-permute-start | bytes 786440 | tf_op jit(solution)/shard_map/ppermute | solution.py:503
  200.9 3.5 %all-to-all-start.11 = ((f32[16,8,128]{2,1,0:T(8,128)}), f32[16,8,128]{2,1,0:T(8,128)S(1)}, u32[]{:S(2)}, u32[]{:S(2)}) async-start(f32[16,8,128]{2,1,0:T(8,128)} %shard_map.87), calls=%async_computation.11 | async-start | bytes 131072 | tf_op jit(solution)/shard_map/all_to_all | solution.py:478
  204.6 6.3 %all-to-all-done.11 = f32[16,8,128]{2,1,0:T(8,128)S(1)} async-done(((f32[16,8,128]{2,1,0:T(8,128)}), f32[16,8,128]{2,1,0:T(8,128)S(1)}, u32[]{:S(2)}, u32[]{:S(2)}) %all-to-all-start.11) | async-done | bytes 65568 | tf_op jit(solution)/shard_map/all_to_all | solution.py:478
  211.7 10.2 %collective-permute-done.6.refs_4_ = f32[32,2048]{1,0:T(8,128)S(1)} collective-permute-done((f32[32,2048]{1,0:T(8,128)}, f32[32,2048]{1,0:T(8,128)S(1)}, u32[]{:S(2)}, u32[]{:S(2)}) %collective-permute-start.6) | collective-permute-done | bytes 262176 | tf_op jit(solution)/shard_map/ppermute | solution.py:503
  226.6 5.4 %all-to-all-start.12 = ((f32[16,8,128]{2,1,0:T(8,128)}), f32[16,8,128]{2,1,0:T(8,128)}, u32[]{:S(2)}, u32[]{:S(2)}) async-start(f32[16,8,128]{2,1,0:T(8,128)} %broadcast_in_dim.17), calls=%async_computation.12 | async-start | bytes 131072 | tf_op jit(solution)/shard_map/all_to_all | solution.py:480
  234.1 5.8 %all-to-all-done.12 = f32[16,8,128]{2,1,0:T(8,128)} async-done(((f32[16,8,128]{2,1,0:T(8,128)}), f32[16,8,128]{2,1,0:T(8,128)}, u32[]{:S(2)}, u32[]{:S(2)}) %all-to-all-start.12) | async-done | bytes 65568 | tf_op jit(solution)/shard_map/all_to_all | solution.py:480
  240.8 4.4 %shard_map.89 = bf16[2,512,2048]{2,1,0:T(8,128)(2,1)} custom-call(f32[8,128]{1,0:T(8,128)S(1)} %broadcast_in_dim.10.scalars.refs_0_, bf16[2,512,2048]{2,1,0:T(8,128)(2,1)} %bitcast.17, bf16[512,128]{1,0:T(8,128)(2,1)S(1)} %bitcast_convert_fusion.u_ref.refs_2_, bf16[16,64,128]{2,1,0:T(8,128)(2,1)S(1)} %all-to-all-done.10.v_ref.refs_3_, ...), custom_call_target="tpu_custom_call" | custom-call | tf_op jit(solution)/shard_map/pallas_call | solution.py:398
  (55 shorter events, 55.9 us)
Async XLA Ops:
  4.7 18.0 %all-to-all-start.2 = ((f32[16,64,128]{2,1,0:T(8,128)}), f32[16,64,128]{2,1,0:T(8,128)S(1)}, u32[]{:S(2)}, u32[]{:S(2)}) async-start(f32[16,64,128]{2,1,0:T(8,128)} %shard_map.76), calls=%async_computation.2 | async-start | bytes 1048576 | tf_op jit(solution)/shard_map/all_to_all | solution.py:428
  25.6 11.3 %all-to-all-start.3 = ((bf16[16,32,128]{2,1,0:T(8,128)(2,1)}), bf16[16,32,128]{2,1,0:T(8,128)(2,1)S(1)}, u32[]{:S(2)}, u32[]{:S(2)}) async-start(bf16[16,32,128]{2,1,0:T(8,128)(2,1)} %shard_map.77), calls=%async_computation.3 | async-start | bytes 262144 | tf_op jit(solution)/shard_map/all_to_all | solution.py:459
  36.9 0.7 copy-start.4
  40.3 3.8 %collective-permute-start = (f32[8,104,128]{2,1,0:T(8,128)S(1)}, f32[8,104,128]{2,1,0:T(8,128)S(1)}, u32[]{:S(2)}, u32[]{:S(2)}) collective-permute-start(f32[8,104,128]{2,1,0:T(8,128)S(1)} %get-tuple-element.57), channel_id=1, source_target_pairs={{0,16},{16,0},{32,48},{48,32},{64,80},{80,64},{96,112},{112,96},{1... | collective-permute-start | bytes 1277960 | tf_op jit(solution)/shard_map/ppermute | solution.py:469
  87.8 17.2 %all-to-all-start.6 = ((f32[16,48,128]{2,1,0:T(8,128)}), f32[16,48,128]{2,1,0:T(8,128)S(1)}, u32[]{:S(2)}, u32[]{:S(2)}) async-start(f32[16,48,128]{2,1,0:T(8,128)} %shard_map.80), calls=%async_computation.6 | async-start | bytes 786432 | tf_op jit(solution)/shard_map/all_to_all | solution.py:492
  113.2 11.9 %all-to-all-start.7 = ((f32[16,32,128]{2,1,0:T(8,128)}), f32[16,32,128]{2,1,0:T(8,128)S(1)}, u32[]{:S(2)}, u32[]{:S(2)}) async-start(f32[16,32,128]{2,1,0:T(8,128)} %get-tuple-element.62), calls=%async_computation.7 | async-start | bytes 524288 | tf_op jit(solution)/shard_map/all_to_all | solution.py:456
  116.7 52.1 %collective-permute-start.2 = (f32[8,32,2048]{2,1,0:T(8,128)}, f32[8,32,2048]{2,1,0:T(8,128)}, u32[]{:S(2)}, u32[]{:S(2)}) collective-permute-start(f32[8,32,2048]{2,1,0:T(8,128)} %get-tuple-element.69), channel_id=1, source_target_pairs={{0,16},{16,0},{32,48},{48,32},{64,80},{80,64},{96,112},{112,96},{1... | collective-permute-start | bytes 6291464 | tf_op jit(solution)/shard_map/ppermute | solution.py:447
  135.4 33.4 %copy-start.2 = (f32[8,32,2048]{2,1,0:T(8,128)S(1)}, f32[8,32,2048]{2,1,0:T(8,128)}, u32[]{:S(2)}) copy-start(f32[8,32,2048]{2,1,0:T(8,128)} %get-tuple-element.68.refs_0_) | copy-start | bytes 6291460
  138.9 4.2 %collective-permute-start.1 = (f32[8,112,128]{2,1,0:T(8,128)S(1)}, f32[8,112,128]{2,1,0:T(8,128)S(1)}, u32[]{:S(2)}, u32[]{:S(2)}) collective-permute-start(f32[8,112,128]{2,1,0:T(8,128)S(1)} %get-tuple-element.66), channel_id=1, source_target_pairs={{0,16},{16,0},{32,48},{48,32},{64,80},{80,64},{96,112},{112,96},{1... | collective-permute-start | bytes 1376264 | tf_op jit(solution)/shard_map/ppermute | solution.py:469
  165.0 31.8 %all-to-all-start.10 = ((bf16[16,64,128]{2,1,0:T(8,128)(2,1)}), bf16[16,64,128]{2,1,0:T(8,128)(2,1)S(1)}, u32[]{:S(2)}, u32[]{:S(2)}) async-start(bf16[16,64,128]{2,1,0:T(8,128)(2,1)} %get-tuple-element.67), calls=%async_computation.10 | async-start | bytes 524288 | tf_op jit(solution)/shard_map/all_to_all | solution.py:474
  171.4 12.2 %collective-permute-start.3 = (f32[32,2048]{1,0:T(8,128)}, f32[32,2048]{1,0:T(8,128)S(1)}, u32[]{:S(2)}, u32[]{:S(2)}) collective-permute-start(f32[32,2048]{1,0:T(8,128)} %get-tuple-element.71), channel_id=1, source_target_pairs={{0,32},{16,48},{32,64},{48,80},{64,96},{80,112},{96,128},{112,144}... | collective-permute-start | bytes 786440 | tf_op jit(solution)/shard_map/ppermute | solution.py:503
  172.8 20.2 %collective-permute-start.4 = (f32[32,2048]{1,0:T(8,128)}, f32[32,2048]{1,0:T(8,128)S(1)}, u32[]{:S(2)}, u32[]{:S(2)}) collective-permute-start(f32[32,2048]{1,0:T(8,128)} %get-tuple-element.72), channel_id=1, source_target_pairs={{0,64},{16,80},{32,96},{48,112},{64,128},{80,144},{96,160},{112,17... | collective-permute-start | bytes 786440 | tf_op jit(solution)/shard_map/ppermute | solution.py:503
  174.9 36.7 %collective-permute-start.5 = (f32[32,2048]{1,0:T(8,128)}, f32[32,2048]{1,0:T(8,128)S(1)}, u32[]{:S(2)}, u32[]{:S(2)}) collective-permute-start(f32[32,2048]{1,0:T(8,128)} %get-tuple-element.73), channel_id=1, source_target_pairs={{0,96},{16,112},{32,128},{48,144},{64,160},{80,176},{96,192},{112,... | collective-permute-start | bytes 786440 | tf_op jit(solution)/shard_map/ppermute | solution.py:503
  177.4 44.5 %collective-permute-start.6 = (f32[32,2048]{1,0:T(8,128)}, f32[32,2048]{1,0:T(8,128)S(1)}, u32[]{:S(2)}, u32[]{:S(2)}) collective-permute-start(f32[32,2048]{1,0:T(8,128)} %get-tuple-element.74), channel_id=1, source_target_pairs={{0,128},{16,144},{32,160},{48,176},{64,192},{80,208},{96,224},{112... | collective-permute-start | bytes 786440 | tf_op jit(solution)/shard_map/ppermute | solution.py:503
  179.4 42.5 %collective-permute-start.7 = (f32[32,2048]{1,0:T(8,128)}, f32[32,2048]{1,0:T(8,128)S(1)}, u32[]{:S(2)}, u32[]{:S(2)}) collective-permute-start(f32[32,2048]{1,0:T(8,128)} %get-tuple-element.75), channel_id=1, source_target_pairs={{0,160},{16,176},{32,192},{48,208},{64,224},{80,240},{96,0},{112,1... | collective-permute-start | bytes 786440 | tf_op jit(solution)/shard_map/ppermute | solution.py:503
  183.6 39.4 %collective-permute-start.8 = (f32[32,2048]{1,0:T(8,128)}, f32[32,2048]{1,0:T(8,128)S(1)}, u32[]{:S(2)}, u32[]{:S(2)}) collective-permute-start(f32[32,2048]{1,0:T(8,128)} %get-tuple-element.76), channel_id=1, source_target_pairs={{0,192},{16,208},{32,224},{48,240},{64,0},{80,16},{96,32},{112,48}... | collective-permute-start | bytes 786440 | tf_op jit(solution)/shard_map/ppermute | solution.py:503
  193.1 33.0 %collective-permute-start.9 = (f32[32,2048]{1,0:T(8,128)}, f32[32,2048]{1,0:T(8,128)S(1)}, u32[]{:S(2)}, u32[]{:S(2)}) collective-permute-start(f32[32,2048]{1,0:T(8,128)} %get-tuple-element.77), channel_id=1, source_target_pairs={{0,224},{16,240},{32,0},{48,16},{64,32},{80,48},{96,64},{112,80},{... | collective-permute-start | bytes 786440 | tf_op jit(solution)/shard_map/ppermute | solution.py:503
  196.8 2.2 copy-start
  199.0 34.0 %copy-start.3 = (f32[32,2048]{1,0:T(8,128)S(1)}, f32[32,2048]{1,0:T(8,128)}, u32[]{:S(2)}) copy-start(f32[32,2048]{1,0:T(8,128)} %get-tuple-element.80.refs_0_) | copy-start | bytes 786436
  200.9 10.0 %all-to-all-start.11 = ((f32[16,8,128]{2,1,0:T(8,128)}), f32[16,8,128]{2,1,0:T(8,128)S(1)}, u32[]{:S(2)}, u32[]{:S(2)}) async-start(f32[16,8,128]{2,1,0:T(8,128)} %shard_map.87), calls=%async_computation.11 | async-start | bytes 131072 | tf_op jit(solution)/shard_map/all_to_all | solution.py:478
  226.6 13.3 %all-to-all-start.12 = ((f32[16,8,128]{2,1,0:T(8,128)}), f32[16,8,128]{2,1,0:T(8,128)}, u32[]{:S(2)}, u32[]{:S(2)}) async-start(f32[16,8,128]{2,1,0:T(8,128)} %broadcast_in_dim.17), calls=%async_computation.12 | async-start | bytes 131072 | tf_op jit(solution)/shard_map/all_to_all | solution.py:480
